TPU v7x, 32 devices: a whole 2x2x4 slice. The times are simulated.
32 devices in a mesh: row: 8 (over z, y), col: 4 (over x, core).
Axes of the slice: x: 2, y: 2, z: 4, core: 2. Of those that a mesh axis runs over, the one named last changes fastest.
Arguments:
- momentum: float32 [8192, 8192], P('row', 'col'), may hold values from -6 to 6
- gradient: bfloat16 [8192, 8192], P('row', 'col'), may hold values from -6 to 6
- weight: bfloat16 [8192, 8192], P('row', 'col'), may hold values from -6 to 6
- right_start: float32 [8192, 512], P('col', 'row'), may hold values from -0.0625 to 0.0625
Outputs:
- new_momentum: float32 [8192, 8192], P('row', 'col')
- new_weight: bfloat16 [8192, 8192], P('row', 'col')
- new_right: float32 [8192, 512], P('col', 'row')
All inputs are finite; a program needn't handle non-finite values.
Results may differ from a plain program's by a relative error of at most 0.001.
Values sent between devices are 32-bit elements; how exact they have to be, the bound alone decides.
A program may use at most 128 MiB of HBM per device.

v0:
```python
import jax
import jax.numpy as jnp
from jax import lax
from jax.sharding import PartitionSpec as P

ITERS = 2
BLOCK = 128


gram_mode = lax.Precision.HIGHEST
wide_mode = lax.Precision.HIGH
momentum_decay = 0.9
step_rate = 0.1
epsilon = 1e-06


def self_gram(rows):
    return lax.dot_general(rows, rows, (((0,), (0,)), ((), ())), precision=gram_mode)


def times_transposed(a, b):
    return lax.dot_general(a, b, (((1,), (1,)), ((), ())), precision=gram_mode)


def solve_rows(rows, gram_sum):
    rank = gram_sum.shape[0]
    block = min(BLOCK, rank)
    trailing = gram_sum
    rest = rows
    solved = []
    for at in range(0, rank, block):
        size = min(block, rank - at)
        corner = lax.linalg.cholesky(trailing[:size, :size], symmetrize_input=False)
        inverse = lax.linalg.triangular_solve(
            corner, jnp.eye(size, dtype=corner.dtype), left_side=True, lower=True
        )
        block_rows = times_transposed(rest[:, :size], inverse)
        solved.append(block_rows)
        if at + size < rank:
            panel = times_transposed(trailing[size:, :size], inverse)
            trailing = trailing[size:, size:] - times_transposed(panel, panel)
            rest = rest[:, size:] - times_transposed(block_rows, panel)
    return jnp.concatenate(solved, axis=1)


def shards(momentum, gradient, weight, right_start):
    rows_at, cols_at = lax.psum(1, "row"), lax.psum(1, "col")
    out_dim, in_dim = momentum.shape[0] * rows_at, momentum.shape[1] * cols_at
    rank = right_start.shape[1] * rows_at
    blended = momentum + gradient.astype(jnp.float32)
    right_full = lax.all_gather(right_start, "row", axis=1, tiled=True)
    right_shard = right_start
    for iteration in range(ITERS):
        partials = jnp.dot(blended, right_full, precision=wide_mode)
        left_sum = lax.psum(partials, "col")
        gram_sum = lax.psum(self_gram(left_sum), "row")
        left_rows = solve_rows(left_sum, gram_sum)
        transposed = lax.dot_general(
            blended, left_rows, (((0,), (0,)), ((), ())), precision=wide_mode
        )
        products = lax.psum_scatter(transposed, "row", scatter_dimension=1, tiled=True)
        squares = lax.psum(jnp.sum(products * products, axis=0, keepdims=True), "col")
        col_norms = jnp.sqrt(squares + epsilon)
        right_shard = products / col_norms
        products_full, norms_full = (
            lax.all_gather(products, "row", axis=1, tiled=True),
            lax.all_gather(col_norms, "row", axis=1, tiled=True),
        )
        right_full = products_full / norms_full
    outer_dims = (((1,), (1,)), ((), ()))
    feedback = lax.dot_general(left_rows, products_full, outer_dims, precision=wide_mode)
    new_momentum = blended - (1.0 - momentum_decay) * feedback
    scale_factor = step_rate * (out_dim * in_dim / rank) ** 0.5
    update = lax.dot_general(left_rows, right_full, outer_dims, precision=wide_mode)
    new_weight = (weight.astype(jnp.float32) - scale_factor * update).astype(jnp.bfloat16)
    return (new_momentum, new_weight, right_shard)


def solution(mesh):
    return jax.shard_map(
        shards,
        mesh=mesh,
        in_specs=(P("row", "col"), P("row", "col"), P("row", "col"), P("col", "row")),
        out_specs=(P("row", "col"), P("row", "col"), P("col", "row")),
        check_vma=False,
    )
```

profile of v0, /device:TPU:13, one launch (start us, length us, event | category | flops | bytes accessed | tf_op | source)
XLA Modules:
  0.0 964.5 jit_solution(15669869728964990464)
XLA Ops:
  7.2 0.7 all-gather.4.cloned.1.call-update
  7.9 73.2 %all-gather.4.cloned.1.call-done = f32[2048,512]{0,1:T(8,128)} async-done(((f32[2048,64]{0,1:T(8,128)}), f32[2048,512]{0,1:T(8,128)}) %all-gather.4.cloned.1.call-update) | async-done | bytes 4194320 | tf_op jit(solution)/shard_map/all_gather | solution.py:51
  81.1 12.0 %fusion.75 = f32[1024,512]{1,0:T(8,128)} fusion(f32[2048,512]{0,1:T(8,128)} %all-gather.4.cloned.1.call-done, f32[1024,2048]{1,0:T(8,128)} %param.7, bf16[1024,2048]{1,0:T(8,128)(2,1)} %param.8), kind=kOutput, calls=%fused_computation.122 | convolution fusion | flops 6446645248 | bytes 18874368 | tf_op jit(solution)/shard_map/dot_general | solution.py:54
  93.1 52.7 %all-reduce.7.cloned.1.call-done = f32[1024,512]{1,0:T(8,128)} async-done(((f32[1024,512]{1,0:T(8,128)}), f32[1024,512]{1,0:T(8,128)}) %all-reduce.7.cloned.1.call-update) | async-done | bytes 2097168 | tf_op jit(solution)/shard_map/psum | solution.py:55
  145.9 6.7 fusion.76
  152.8 77.4 %all-reduce.9.cloned.1.call-done = f32[512,512]{1,0:T(8,128)} async-done(((f32[512,512]{1,0:T(8,128)}), f32[512,512]{1,0:T(8,128)}) %all-reduce.9.cloned.1.call-update) | async-done | bytes 1048592 | tf_op jit(solution)/shard_map/psum | solution.py:56
  230.3 0.8 slice.125
  231.1 11.7 %custom-call.20 = f32[128,128]{1,0:T(8,128)S(1)} custom-call(f32[128,128]{1,0:T(8,128)S(1)} %slice.125), custom_call_target="Cholesky" | custom-call | tf_op jit(solution)/shard_map/cholesky/custom-call.1 | solution.py:33
  242.8 0.6 compare_reduce_fusion.7
  243.5 0.7 fusion.50
  244.2 9.8 %custom-call.21 = f32[1,128,128]{1,2,0:T(8,128)S(1)} custom-call(f32[1,128,128]{2,1,0:T(8,128)S(1)} %fusion.50), custom_call_target="InvertDiagBlocksLowerTriangular" | custom-call | tf_op jit(solution)/shard_map/triangular_solve/custom-call.0 | solution.py:34
  254.3 1.3 fusion.44
  255.5 1.7 convolution_subtract_fusion.3
  257.2 11.7 %custom-call.22 = f32[128,128]{1,0:T(8,128)S(1)} custom-call(f32[128,128]{1,0:T(8,128)S(1)} %slice.130), custom_call_target="Cholesky" | custom-call | tf_op jit(solution)/shard_map/cholesky/custom-call.1 | solution.py:33
  269.0 0.6 compare_reduce_fusion.6
  269.6 0.7 fusion.51
  270.3 10.2 %custom-call.23 = f32[1,128,128]{1,2,0:T(8,128)S(1)} custom-call(f32[1,128,128]{2,1,0:T(8,128)S(1)} %fusion.51), custom_call_target="InvertDiagBlocksLowerTriangular" | custom-call | tf_op jit(solution)/shard_map/triangular_solve/custom-call.0 | solution.py:34
  281.5 11.7 %custom-call.24 = f32[128,128]{1,0:T(8,128)S(1)} custom-call(f32[128,128]{1,0:T(8,128)S(1)} %slice.135), custom_call_target="Cholesky" | custom-call | tf_op jit(solution)/shard_map/cholesky/custom-call.1 | solution.py:33
  293.8 0.7 fusion.52
  294.5 9.8 %custom-call.25 = f32[1,128,128]{1,2,0:T(8,128)S(1)} custom-call(f32[1,128,128]{2,1,0:T(8,128)S(1)} %fusion.52), custom_call_target="InvertDiagBlocksLowerTriangular" | custom-call | tf_op jit(solution)/shard_map/triangular_solve/custom-call.0 | solution.py:34
  305.2 11.7 %custom-call.26 = f32[128,128]{1,0:T(8,128)S(1)} custom-call(f32[128,128]{1,0:T(8,128)S(1)} %convolution_subtract_fusion.9), custom_call_target="Cholesky" | custom-call | tf_op jit(solution)/shard_map/cholesky/custom-call.1 | solution.py:33
  317.6 0.7 fusion.53
  318.2 10.0 %custom-call.27 = f32[1,128,128]{1,2,0:T(8,128)S(1)} custom-call(f32[1,128,128]{2,1,0:T(8,128)S(1)} %fusion.53), custom_call_target="InvertDiagBlocksLowerTriangular" | custom-call | tf_op jit(solution)/shard_map/triangular_solve/custom-call.0 | solution.py:34
  329.1 1.9 slice_subtract_fusion.1
  331.7 1.1 convolution_subtract_fusion.1
  333.3 1.0 convolution_subtract_fusion.5
  335.0 11.1 %fusion.3 = f32[2048,512]{0,1:T(8,128)} fusion(f32[1024,128]{0,1:T(8,128)S(1)} %fusion.77, f32[1024,128]{0,1:T(8,128)S(1)} %fusion.19, f32[1024,128]{0,1:T(8,128)S(1)} %fusion.21, f32[1024,128]{0,1:T(8,128)S(1)} %fusion.23, f32[1024,2048]{1,0:T(8,128)} %param.7, bf16[1024,2048]{1,0:T(8,128)(2,1)S(1)} %copy-done), kind=kOutput, calls=%fused_computation.6 | convolution fusion | flops 6448218112 | bytes 18874368 | tf_op jit(solution)/shard_map/dot_general | solution.py:58
  346.1 88.9 %reduce-scatter.3.cloned.1.call-done = f32[2048,64]{0,1:T(8,128)} async-done(((f32[2048,512]{0,1:T(8,128)}), f32[2048,64]{0,1:T(8,128)}) %reduce-scatter.3.cloned.1.call-update) | async-done | bytes 524304 | tf_op jit(solution)/shard_map/reduce_scatter | solution.py:61
  436.3 1.2 multiply_reduce_fusion.1
  437.5 6.1 psum.44
  443.7 12.7 %all-reduce = f32[512]{0:T(512)S(1)} all-reduce(f32[512]{0:T(512)S(1)} %bitcast_dynamic-update-slice_fusion), channel_id=1, replica_groups=mesh['row'=8,'col'=4] {'row'}, use_global_device_ids=true, to_apply=%add | all-reduce | flops 512 | bytes 4096
  456.4 50.6 %all-gather.6.cloned.1.call-done = f32[2048,512]{0,1:T(8,128)} async-done(((f32[2048,64]{0,1:T(8,128)}), f32[2048,512]{0,1:T(8,128)}) %all-gather.6.cloned.1.call-update) | async-done | bytes 4194320 | tf_op jit(solution)/shard_map/all_gather | solution.py:66
  507.0 12.2 %fusion.1 = f32[1024,512]{1,0:T(8,128)} fusion(f32[2048,512]{0,1:T(8,128)} %all-gather.6.cloned.1.call-done, f32[512]{0:T(512)S(1)} %all-reduce, f32[1024,2048]{1,0:T(8,128)} %param.7, bf16[1024,2048]{1,0:T(8,128)(2,1)} %param.8), kind=kOutput, calls=%fused_computation.4 | convolution fusion | flops 6447693824 | bytes 18876416 | tf_op jit(solution)/shard_map/dot_general | solution.py:54
  519.2 52.7 %all-reduce.11.cloned.1.call-done = f32[1024,512]{1,0:T(8,128)} async-done(((f32[1024,512]{1,0:T(8,128)}), f32[1024,512]{1,0:T(8,128)}) %all-reduce.11.cloned.1.call-update) | async-done | bytes 2097168 | tf_op jit(solution)/shard_map/psum | solution.py:55
  572.0 6.7 fusion.78
  579.1 77.2 %all-reduce.13.cloned.1.call-done = f32[512,512]{1,0:T(8,128)} async-done(((f32[512,512]{1,0:T(8,128)}), f32[512,512]{1,0:T(8,128)}) %all-reduce.13.cloned.1.call-update) | async-done | bytes 1048592 | tf_op jit(solution)/shard_map/psum | solution.py:56
  656.3 0.8 slice.140
  657.2 11.7 %custom-call.28 = f32[128,128]{1,0:T(8,128)S(1)} custom-call(f32[128,128]{1,0:T(8,128)S(1)} %slice.140), custom_call_target="Cholesky" | custom-call | tf_op jit(solution)/shard_map/cholesky/custom-call.1 | solution.py:33
  669.6 0.7 fusion.54
  670.2 9.8 %custom-call.29 = f32[1,128,128]{1,2,0:T(8,128)S(1)} custom-call(f32[1,128,128]{2,1,0:T(8,128)S(1)} %fusion.54), custom_call_target="InvertDiagBlocksLowerTriangular" | custom-call | tf_op jit(solution)/shard_map/triangular_solve/custom-call.0 | solution.py:34
  680.4 1.3 fusion.42
  681.6 1.7 convolution_subtract_fusion.2
  683.4 11.7 %custom-call.30 = f32[128,128]{1,0:T(8,128)S(1)} custom-call(f32[128,128]{1,0:T(8,128)S(1)} %slice.145), custom_call_target="Cholesky" | custom-call | tf_op jit(solution)/shard_map/cholesky/custom-call.1 | solution.py:33
  695.7 0.7 fusion.55
  696.4 10.0 %custom-call.31 = f32[1,128,128]{1,2,0:T(8,128)S(1)} custom-call(f32[1,128,128]{2,1,0:T(8,128)S(1)} %fusion.55), custom_call_target="InvertDiagBlocksLowerTriangular" | custom-call | tf_op jit(solution)/shard_map/triangular_solve/custom-call.0 | solution.py:34
  708.0 11.7 %custom-call.32 = f32[128,128]{1,0:T(8,128)S(1)} custom-call(f32[128,128]{1,0:T(8,128)S(1)} %slice.150), custom_call_target="Cholesky" | custom-call | tf_op jit(solution)/shard_map/cholesky/custom-call.1 | solution.py:33
  719.7 0.6 compare_reduce_fusion.1
  721.0 9.8 %custom-call.33 = f32[1,128,128]{1,2,0:T(8,128)S(1)} custom-call(f32[1,128,128]{2,1,0:T(8,128)S(1)} %fusion.56), custom_call_target="InvertDiagBlocksLowerTriangular" | custom-call | tf_op jit(solution)/shard_map/triangular_solve/custom-call.0 | solution.py:34
  731.7 11.7 %custom-call.34 = f32[128,128]{1,0:T(8,128)S(1)} custom-call(f32[128,128]{1,0:T(8,128)S(1)} %convolution_subtract_fusion.8), custom_call_target="Cholesky" | custom-call | tf_op jit(solution)/shard_map/cholesky/custom-call.1 | solution.py:33
  743.4 0.6 compare_reduce_fusion
  744.9 9.8 %custom-call.35 = f32[1,128,128]{1,2,0:T(8,128)S(1)} custom-call(f32[1,128,128]{2,1,0:T(8,128)S(1)} %fusion.57), custom_call_target="InvertDiagBlocksLowerTriangular" | custom-call | tf_op jit(solution)/shard_map/triangular_solve/custom-call.0 | solution.py:34
  755.0 1.4 fusion.17
  756.5 1.9 slice_subtract_fusion
  759.0 1.0 convolution_subtract_fusion
  760.7 1.0 convolution_subtract_fusion.4
  762.3 10.9 %fusion.25 = f32[2048,512]{0,1:T(8,128)} fusion(f32[1024,128]{0,1:T(8,128)S(1)} %fusion.79, f32[1024,128]{0,1:T(8,128)S(1)} %fusion.13, f32[1024,128]{0,1:T(8,128)S(1)} %fusion.15, f32[1024,128]{0,1:T(8,128)S(1)} %fusion.17, f32[1024,2048]{1,0:T(8,128)} %param.7, bf16[1024,2048]{1,0:T(8,128)(2,1)S(1)} %copy-done.1), kind=kOutput, calls=%fused_computation.43 | convolution fusion | flops 6448218112 | bytes 18874368 | tf_op jit(solution)/shard_map/dot_general | solution.py:58
  773.3 88.9 %reduce-scatter.5.cloned.1.call-done = f32[2048,64]{0,1:T(8,128)} async-done(((f32[2048,512]{0,1:T(8,128)}), f32[2048,64]{0,1:T(8,128)}) %reduce-scatter.5.cloned.1.call-update) | async-done | bytes 524304 | tf_op jit(solution)/shard_map/reduce_scatter | solution.py:61
  862.2 1.2 multiply_reduce_fusion
  863.4 6.1 psum.47
  869.6 12.7 %all-reduce.1 = f32[512]{0:T(512)S(1)} all-reduce(f32[512]{0:T(512)S(1)} %fusion.74), channel_id=1, replica_groups=mesh['row'=8,'col'=4] {'row'}, use_global_device_ids=true, to_apply=%add.1 | all-reduce | flops 512 | bytes 4096
  882.3 1.9 broadcast_divide_fusion
  884.2 50.1 %all-gather.8.cloned.1.call-done = f32[2048,512]{0,1:T(8,128)} async-done(((f32[2048,64]{0,1:T(8,128)}), f32[2048,512]{0,1:T(8,128)}) %all-gather.8.cloned.1.call-update) | async-done | bytes 4194320 | tf_op jit(solution)/shard_map/all_gather | solution.py:66
  934.3 13.9 %multiply_subtract_fusion = f32[1024,2048]{1,0:T(8,128)} fusion(f32[2048,512]{0,1:T(8,128)} %all-gather.8.cloned.1.call-done, f32[1024,128]{0,1:T(8,128)S(1)} %fusion.79, f32[1024,128]{0,1:T(8,128)S(1)} %fusion.13, f32[1024,128]{0,1:T(8,128)S(1)} %fusion.15, f32[1024,128]{0,1:T(8,128)S(1)} %fusion.17, f32[1024,2048]{1,0:T(8,128)} %param.7, ...), kind=kOutput, calls=%fused_computation.1 | convolution fusion | flops 6452412416 | bytes 27262976 | tf_op jit(solution)/shard_map/dot_general | solution.py:71
  948.3 9.3 subtract_convert_fusion
  (84 shorter events, 15.6 us)
Async XLA Ops:
  7.2 73.9 %all-gather.4.cloned.1.call-start = ((), (), s32[]{:S(2)}) async-start(), calls=%async_computation.2 | async-start | bytes 4718592 | tf_op jit(solution)/shard_map/all_gather | solution.py:51
  7.9 138.0 %all-reduce.7.cloned.1.call-start = ((), (), s32[]{:S(2)}) async-start(), calls=%async_computation.3 | async-start | bytes 4194304 | tf_op jit(solution)/shard_map/psum | solution.py:55
  93.1 137.2 %all-reduce.9.cloned.1.call-start = ((), (), s32[]{:S(2)}) async-start(), calls=%async_computation.4 | async-start | bytes 2097152 | tf_op jit(solution)/shard_map/psum | solution.py:56
  152.6 175.9 %copy-start.2 = (f32[1024,512]{1,0:T(8,128)S(1)}, f32[1024,512]{1,0:T(8,128)}, u32[]{:S(2)}) copy-start(f32[1024,512]{1,0:T(8,128)} %all-reduce.7.cloned.1.call-done) | copy-start | bytes 6291460
  152.6 282.4 %reduce-scatter.3.cloned.1.call-start = ((), (), s32[]{:S(2)}) async-start(), calls=%async_computation.5 | async-start | bytes 4718592 | tf_op jit(solution)/shard_map/reduce_scatter | solution.py:61
  331.0 3.9 copy-start
  346.0 89.1 %copy-start.9 = (u32[32]{0:T(128)S(1)}, u32[32]{0:T(128)}, u32[]{:S(2)}) copy-start(u32[32]{0:T(128)} %constant.27) | copy-start | bytes 388
  346.1 161.0 %all-gather.6.cloned.1.call-start = ((), (), s32[]{:S(2)}) async-start(), calls=%async_computation.6 | async-start | bytes 4718592 | tf_op jit(solution)/shard_map/all_gather | solution.py:66
  435.0 136.9 %all-reduce.11.cloned.1.call-start = ((), (), s32[]{:S(2)}) async-start(), calls=%async_computation.7 | async-start | bytes 4194304 | tf_op jit(solution)/shard_map/psum | solution.py:55
  519.2 137.1 %all-reduce.13.cloned.1.call-start = ((), (), s32[]{:S(2)}) async-start(), calls=%async_computation.8 | async-start | bytes 2097152 | tf_op jit(solution)/shard_map/psum | solution.py:56
  578.6 176.4 %copy-start.3 = (f32[1024,512]{1,0:T(8,128)S(1)}, f32[1024,512]{1,0:T(8,128)}, u32[]{:S(2)}) copy-start(f32[1024,512]{1,0:T(8,128)} %all-reduce.11.cloned.1.call-done) | copy-start | bytes 6291460
  578.7 283.5 %reduce-scatter.5.cloned.1.call-start = ((), (), s32[]{:S(2)}) async-start(), calls=%async_computation.9 | async-start | bytes 4718592 | tf_op jit(solution)/shard_map/reduce_scatter | solution.py:61
  680.3 26.3 %copy-start.5 = (f32[128,128]{1,0:T(8,128)}, f32[128,128]{1,0:T(8,128)S(1)}, u32[]{:S(2)}) copy-start(f32[128,128]{1,0:T(8,128)S(1)} %fusion.32) | copy-start | bytes 196612
  706.7 0.6 copy-start.6
  708.0 50.4 %copy-start.7 = (f32[128,128]{1,0:T(8,128)S(1)}, f32[128,128]{1,0:T(8,128)}, u32[]{:S(2)}) copy-start(f32[128,128]{1,0:T(8,128)} %copy-done.6) | copy-start | bytes 196612
  758.4 3.9 copy-start.1
  773.2 161.1 %all-gather.8.cloned.1.call-start = ((), (), s32[]{:S(2)}) async-start(), calls=%async_computation.10 | async-start | bytes 4718592 | tf_op jit(solution)/shard_map/all_gather | solution.py:66
  934.3 13.9 %copy-start.4 = (f32[2048,512]{0,1:T(8,128)S(1)}, f32[2048,512]{0,1:T(8,128)}, u32[]{:S(2)}) copy-start(f32[2048,512]{0,1:T(8,128)} %all-gather.8.cloned.1.call-done) | copy-start | bytes 12582916
  934.3 13.9 %copy-start.8 = (bf16[1024,2048]{1,0:T(8,128)(2,1)S(1)}, bf16[1024,2048]{1,0:T(8,128)(2,1)}, u32[]{:S(2)}) copy-start(bf16[1024,2048]{1,0:T(8,128)(2,1)} %param.9) | copy-start | bytes 12582916
Sparse Core Ops, SparseCore 0:
  10.1 70.9 all-gather.3
  93.2 52.6 all-reduce.6
  152.7 77.5 all-reduce.8
  346.2 88.7 reduce-scatter.2
  437.0 69.9 all-gather.5
  519.3 52.5 all-reduce.10
  578.8 77.5 all-reduce.12
  773.3 88.8 reduce-scatter.4
  864.3 69.9 all-gather.7
where the time goes:
time: 975 us; the launch traced here: 965 us
  waiting for transfers between devices  613 us (63%)
  other arithmetic  188 us (19%)
  matrix products  107 us (11%)
  blocking collectives  37.6 us (4%)
  between operations  15.6 us (2%)
    reduce_scatter x2, waiting for transfers between devices, shards(): lax.psum_scatter(transposed, 'row', scatter_dimension=1, tiled=True)  178 us
    psum x2, waiting for transfers between devices, shards(): gram_sum = lax.psum(self_gram(left_sum), 'row')  155 us
    psum x2, waiting for transfers between devices, shards(): left_sum = lax.psum(partials, 'col')  105 us
    all_gather x2, waiting for transfers between devices, shards(): lax.all_gather(products, 'row', axis=1, tiled=True)  101 us
    another operation x24, other arithmetic, solve_rows(): corner = lax.linalg.cholesky(trailing[:size, :size], symmetrize_input=False)  99.1 us
    another operation x16, other arithmetic, solve_rows(): lax.linalg.triangular_solve(corner, jnp.eye(size, dtype=corner.dtype), le...  84.4 us
    all_gather x1, waiting for transfers between devices, shards(): right_full = lax.all_gather(right_start, 'row', axis=1, tiled=True)  73.2 us
    unnamed x2, blocking collectives  25.4 us
  transfers between devices with their start and end apart: 9, of which 9 were waited for; matrix products, arithmetic and copies ran while one was open for 1% of the time, Pallas kernels for 0%

commit v1 on v0

v1 whole, which is shorter than its diff:
```python
import functools

import jax
import jax.numpy as jnp
from jax import lax
from jax.experimental import pallas as pl
from jax.experimental.pallas import tpu as pltpu
from jax.sharding import PartitionSpec as P

ITERS = 2
CORES = 2
momentum_decay = 0.9
step_rate = 0.1
epsilon = 1e-06
exact = lax.Precision.HIGHEST
f32, bf16 = jnp.float32, jnp.bfloat16
VMEM = pl.BlockSpec(memory_space=pltpu.VMEM)
MESH = pl.DeviceIdType.MESH
LIMIT = 56 << 20


def nt(a, b, precision=None):
    return lax.dot_general(a, b, (((1,), (1,)), ((), ())), precision=precision, preferred_element_type=f32)


def nn(a, b, precision=None):
    return lax.dot_general(a, b, (((1,), (0,)), ((), ())), precision=precision, preferred_element_type=f32)


def split(x):
    high = x.astype(bf16)
    return high, (x - high.astype(f32)).astype(bf16)


def three(dot, a, b):
    return (dot(a[1], b[0]) + dot(a[0], b[1])) + dot(a[0], b[0])


def outer_factor(n):
    d = 1
    while d * d < n or n % d:
        d += 1
    return d


def cost(flops, moved):
    return pl.CostEstimate(flops=int(flops), bytes_accessed=int(moved), transcendentals=0)


def eye(n):
    return (lax.broadcasted_iota(jnp.int32, (n, n), 0) == lax.broadcasted_iota(jnp.int32, (n, n), 1)).astype(f32)


def eliminate(a, w):
    size = a.shape[0]
    shape = (8, size)
    sub = lax.broadcasted_iota(jnp.int32, shape, 0)
    w[...] = eye(size)
    for at in range(0, size, 8):
        slab, inv_rows = a[at : at + 8, :], w[at : at + 8, :]
        cols = [jnp.broadcast_to(slab[:, at + i : at + i + 1], shape) for i in range(8)]
        scale = jnp.zeros(shape, f32)
        for i in range(8):
            pivot = jnp.broadcast_to(cols[i][i : i + 1, :], shape)
            scale = jnp.where(sub == i, lax.rsqrt(pivot), scale)
            if i < 7:
                m = jnp.where(sub > i, cols[i] / pivot, 0.0)
                for k in range(i + 1, 8):
                    cols[k] = cols[k] - m * jnp.broadcast_to(cols[k][i : i + 1, :], shape)
                slab = slab - m * jnp.broadcast_to(slab[i : i + 1, :], shape)
                inv_rows = inv_rows - m * jnp.broadcast_to(inv_rows[i : i + 1, :], shape)
        upper, inv_rows = slab * scale, inv_rows * scale
        w[at : at + 8, :] = inv_rows
        lower = upper.T
        for k in range(at + 8, size, 8):
            rows, inv = a[k : k + 8, :], w[k : k + 8, :]
            for i in range(8):
                factor = jnp.broadcast_to(lower[k : k + 8, i : i + 1], shape)
                rows = rows - factor * jnp.broadcast_to(upper[i : i + 1, :], shape)
                inv = inv - factor * jnp.broadcast_to(inv_rows[i : i + 1, :], shape)
            a[k : k + 8, :] = rows
            w[k : k + 8, :] = inv


def factor_kernel(gram, x, work, a, w):
    rank, block = gram.shape[0], a.shape[0]
    work[...] = gram[...]
    x[...] = eye(rank)
    for at in range(0, rank, block):
        end = at + block
        a[...] = work[at:end, at:end]
        eliminate(a, w)
        inverse = w[...]
        x[at:end, :] = nn(inverse, x[at:end, :], exact)
        if end < rank:
            panel = nt(work[end:, at:end], inverse, exact)
            work[end:, end:] = work[end:, end:] - nt(panel, panel, exact)
            x[end:, :] = x[end:, :] - nn(panel, x[at:end, :], exact)


def inverse_factor(gram):
    rank = gram.shape[0]
    block = min(128, rank)
    return pl.pallas_call(
        factor_kernel,
        name="factor",
        out_shape=jax.ShapeDtypeStruct((rank, rank), f32),
        in_specs=[VMEM],
        out_specs=VMEM,
        scratch_shapes=[pltpu.VMEM((rank, rank), f32)] + [pltpu.VMEM((block, block), f32)] * 2,
        cost_estimate=cost(2e10, 2 << 20),
    )(gram)


def prep_kernel(m, g, high, low):
    high[...], low[...] = split(m[...] + g[...].astype(f32))


def prepare(momentum, gradient):
    rows, cols = momentum.shape
    tile = min(256, rows)
    spec = pl.BlockSpec((tile, cols), lambda i: (i, 0))
    shape = jax.ShapeDtypeStruct((rows, cols), bf16)
    return pl.pallas_call(
        prep_kernel,
        name="prepare",
        grid=(rows // tile,),
        in_specs=[spec, spec],
        out_specs=[spec, spec],
        out_shape=[shape, shape],
        cost_estimate=cost(2 * rows * cols, 10 * rows * cols),
    )(momentum, gradient)


def first_kernel(r, high, low, out):
    part = three(nt, split(r[...]), (high[...], low[...]))
    step = pl.program_id(0)

    @pl.when(step == 0)
    def _():
        out[...] = part

    @pl.when(step > 0)
    def _():
        out[...] = out[...] + part


def row_sums(total):
    rank = total.shape[0]
    column = jnp.sum(total, axis=1, keepdims=True)
    return jnp.broadcast_to(column, (rank, 128)).T[:8, :]


def solved_kernel(multiply, x, q, *refs):
    if multiply:
        high, low, solved, squares, out, total = refs
    else:
        solved, squares, total = refs
    s = three(nn, split(x[...]), split(q[...]))
    solved[...] = s
    sums = s[:, :128] * s[:, :128]
    for at in range(128, s.shape[1], 128):
        sums = sums + s[:, at : at + 128] * s[:, at : at + 128]
    step = pl.program_id(0)

    @pl.when(step == 0)
    def _():
        total[...] = sums

    @pl.when(step > 0)
    def _():
        total[...] = total[...] + sums

    if multiply:
        part = three(nt, split(s), (high[...], low[...]))

        @pl.when(step == 0)
        def _():
            out[...] = part

        @pl.when(step > 0)
        def _():
            out[...] = out[...] + part

    @pl.when(step == pl.num_programs(0) - 1)
    def _():
        squares[...] = row_sums(total[...])


def first_product(right, high, low):
    rank, (rows, cols) = right.shape[0], high.shape
    wide = min(512, cols)
    block = pl.BlockSpec((rows, wide), lambda j: (0, j))
    return pl.pallas_call(
        first_kernel,
        name="first",
        grid=(cols // wide,),
        in_specs=[pl.BlockSpec((rank, wide), lambda j: (0, j)), block, block],
        out_specs=pl.BlockSpec((rank, rows), lambda j: (0, 0)),
        out_shape=jax.ShapeDtypeStruct((rank, rows), f32),
        compiler_params=pltpu.CompilerParams(vmem_limit_bytes=LIMIT),
        cost_estimate=cost(6 * rank * rows * cols, 4 * rows * cols),
    )(right, high, low)


def solved_product(x, q, high=None, low=None):
    rank, cols = q.shape
    wide = min(512, cols)
    block = pl.BlockSpec((rank, wide), lambda j: (0, j))
    in_specs = [pl.BlockSpec((rank, rank), lambda j: (0, 0)), block]
    out_specs = [block, pl.BlockSpec((8, rank), lambda j: (0, 0))]
    out_shape = [jax.ShapeDtypeStruct((rank, cols), f32), jax.ShapeDtypeStruct((8, rank), f32)]
    args = [x, q]
    if high is not None:
        rows = high.shape[0]
        in_specs += [pl.BlockSpec((rows, wide), lambda j: (0, j))] * 2
        out_specs.append(pl.BlockSpec((rank, rows), lambda j: (0, 0)))
        out_shape.append(jax.ShapeDtypeStruct((rank, rows), f32))
        args += [high, low]
    return pl.pallas_call(
        functools.partial(solved_kernel, high is not None),
        name="solved",
        grid=(cols // wide,),
        in_specs=in_specs,
        out_specs=out_specs,
        out_shape=out_shape,
        scratch_shapes=[pltpu.VMEM((rank, 128), f32)],
        compiler_params=pltpu.CompilerParams(vmem_limit_bytes=LIMIT),
        cost_estimate=cost(12 * rank * rank * cols, 8 * rank * cols),
    )(*args)


def left_kernel(x, p, high, low):
    s = three(nn, split(x[...]), split(p[...])).T
    high[...], low[...] = split(s)


def left_factor(x, p):
    rank, rows = p.shape
    wide = min(256, rows)
    block = pl.BlockSpec((wide, rank), lambda j: (j, 0))
    shape = jax.ShapeDtypeStruct((rows, rank), bf16)
    return pl.pallas_call(
        left_kernel,
        name="left",
        grid=(rows // wide,),
        in_specs=[pl.BlockSpec((rank, rank), lambda j: (0, 0)), pl.BlockSpec((rank, wide), lambda j: (0, j))],
        out_specs=[block, block],
        out_shape=[shape, shape],
        compiler_params=pltpu.CompilerParams(vmem_limit_bytes=LIMIT),
        cost_estimate=cost(6 * rank * rank * rows, 8 * rank * rows),
    )(x, p)


def final_kernel(scale_factor, high, low, q, norms, m, g, weight, new_m, new_w):
    rank = q.shape[0]
    column = jnp.broadcast_to(norms[0:1, :], (128, rank)).T[:, 0:1]
    s = q[...]
    left = (high[...], low[...])
    blended = m[...] + g[...].astype(f32)
    new_m[...] = blended - (1.0 - momentum_decay) * nn(left[0], s.astype(bf16))
    update = three(nn, left, split(s / column))
    new_w[...] = (weight[...].astype(f32) - scale_factor * update).astype(bf16)


def outputs(scale_factor, high, low, q, norms, momentum, gradient, weight):
    rank, cols = q.shape
    rows = high.shape[0]
    wide = min(256, cols)
    side = pl.BlockSpec((rows, rank), lambda j: (0, 0))
    block = pl.BlockSpec((rows, wide), lambda j: (0, j))
    return pl.pallas_call(
        functools.partial(final_kernel, scale_factor),
        name="outputs",
        grid=(cols // wide,),
        in_specs=[side, side, pl.BlockSpec((rank, wide), lambda j: (0, j)), pl.BlockSpec((8, rank), lambda j: (0, 0)), block, block, block],
        out_specs=[block, block],
        out_shape=[jax.ShapeDtypeStruct((rows, cols), f32), jax.ShapeDtypeStruct((rows, cols), bf16)],
        compiler_params=pltpu.CompilerParams(vmem_limit_bytes=LIMIT),
        cost_estimate=cost(8 * rank * rows * cols, 14 * rows * cols),
    )(high, low, q, norms, momentum, gradient, weight)


class Place:
    def __init__(self, rows, cols):
        self.deep = outer_factor(rows)
        self.flat = rows // self.deep
        self.wide = cols // CORES
        self.row, self.col = lax.axis_index("row"), lax.axis_index("col")
        self.z, self.y = self.row // self.flat, self.row % self.flat
        self.x, self.core = self.col // CORES, self.col % CORES

    def to_y(self, d):
        return (self.z * self.flat + (self.y + d) % self.flat, self.col)

    def to_z(self, d):
        return (((self.z + d) % self.deep) * self.flat + self.y, self.col)

    def to_x(self, d):
        return (self.row, ((self.x + d) % self.wide) * CORES + self.core)

    def partner(self):
        return (self.row, self.x * CORES + 1 - self.core)

    def y_peers(self):
        return [self.to_y(d) for d in range(1, self.flat)]

    def z_peers(self):
        return [self.to_z(d) for d in range(1, self.deep)]

    def x_peers(self):
        return [self.to_x(d) for d in range(1, self.wide)]


def greet(peers):
    barrier = pltpu.get_barrier_semaphore()
    for peer in peers:
        pl.semaphore_signal(barrier, inc=1, device_id=peer, device_id_type=MESH)
    pl.semaphore_wait(barrier, len(peers))


class Sender:
    def __init__(self, send, recv):
        self.send, self.recv, self.copies = send, recv, []

    def start(self, src, dst, peer):
        at = len(self.copies)
        copy = pltpu.make_async_remote_copy(
            src_ref=src, dst_ref=dst, send_sem=self.send.at[at], recv_sem=self.recv.at[at], device_id=peer, device_id_type=MESH
        )
        copy.start()
        self.copies.append(copy)
        return copy

    def drain(self):
        for copy in self.copies:
            copy.wait_send()


def join_kernel(rows, cols, pieces, scaled, *refs):
    if scaled:
        p, sq, out, gram, norms, half, near, far, sq_in, send, recv = refs
    else:
        p, out, gram, half, near, far, send, recv = refs
    at = Place(rows, cols)
    greet([at.partner()] + at.x_peers() + ([(at.row, (at.x + d) % at.wide * CORES + 1 - at.core) for d in range(1, at.wide)] if scaled else []))
    go = Sender(send, recv)
    mine, other = at.core, 1 - at.core
    squares = []
    if scaled:
        for d in range(1, cols):
            squares.append(go.start(sq, sq_in.at[d - 1], (at.row, (at.col + d) % cols)))
    first = [go.start(p.at[other, k], near.at[k], at.partner()) for k in range(pieces)]
    second = []
    for k in range(pieces):
        first[k].wait_recv()
        half[k] = p[mine, k] + near[k]
        second.append([go.start(half.at[k], far.at[d, k], peer) for d, peer in enumerate(at.x_peers())])
    if scaled:
        total = sq[...]
        for d, copy in enumerate(squares):
            copy.wait_recv()
            total = total + sq_in[d]
        norm = jnp.sqrt(total + epsilon)
        norms[...] = norm
        rank = norm.shape[1]
        column = jnp.broadcast_to(norm[0:1, :], (128, rank)).T[:, 0:1]
        size = rank // (CORES * pieces)
        columns = [column[k * size : (k + 1) * size] for k in range(CORES * pieces)]
    third = []
    for k in range(pieces):
        total = half[k]
        for d, copy in enumerate(second[k]):
            copy.wait_recv()
            total = total + far[d, k]
        if scaled:
            total = total / jnp.where(mine == 0, columns[k], columns[pieces + k])
        out[mine, k] = total
        third.append(go.start(out.at[mine, k], out.at[mine, k], at.partner()))
    for copy in third:
        copy.wait_recv()
    full = out[...].reshape(-1, p.shape[-1])
    share = gram.shape[0]
    own = p.shape[2] // share if share < p.shape[2] else 1
    if share <= p.shape[2]:
        piece = at.col // own
        lines = out[piece // pieces, piece % pieces, pl.ds(pl.multiple_of((at.col % own) * share, share), share), :]
    else:
        span = share // p.shape[2]
        lines = out[at.col * span // pieces, pl.ds((at.col * span) % pieces, span)].reshape(share, p.shape[-1])
    gram[...] = nt(lines, full, exact)
    go.drain()


def join(part, squares, rows, cols, ident):
    rank, lines = part.shape
    pieces = 4
    size = rank // (CORES * pieces)
    scaled = squares is not None
    wide = cols // CORES
    sends = 2 * pieces + pieces * (wide - 1) + (cols - 1 if scaled else 0)
    out_shape = [jax.ShapeDtypeStruct((CORES, pieces, size, lines), f32), jax.ShapeDtypeStruct((rank // cols, rank), f32)]
    scratch = [pltpu.VMEM((pieces, size, lines), f32)] * 2 + [pltpu.VMEM((wide - 1, pieces, size, lines), f32)]
    args = [part.reshape(CORES, pieces, size, lines)]
    if scaled:
        out_shape.append(jax.ShapeDtypeStruct(squares.shape, f32))
        scratch.append(pltpu.VMEM((cols - 1,) + squares.shape, f32))
        args.append(squares)
    res = pl.pallas_call(
        functools.partial(join_kernel, rows, cols, pieces, scaled),
        name="join",
        out_shape=out_shape,
        in_specs=[VMEM] * len(args),
        out_specs=[VMEM] * len(out_shape),
        scratch_shapes=scratch + [pltpu.SemaphoreType.DMA((sends,))] * 2,
        compiler_params=pltpu.CompilerParams(collective_id=ident, has_side_effects=True, vmem_limit_bytes=LIMIT),
        cost_estimate=cost(6e9, 6 << 20),
    )(*args)
    return [res[0].reshape(rank, lines)] + list(res[1:])


def norm_kernel(rows, cols, sq, norms, sq_in, send, recv):
    at = Place(rows, cols)
    peers = [(at.row, (at.col + d) % cols) for d in range(1, cols)]
    greet(peers)
    go = Sender(send, recv)
    copies = [go.start(sq, sq_in.at[d], peer) for d, peer in enumerate(peers)]
    total = sq[...]
    for d, copy in enumerate(copies):
        copy.wait_recv()
        total = total + sq_in[d]
    norms[...] = jnp.sqrt(total + epsilon)
    go.drain()


def column_norms(squares, rows, cols, ident):
    return pl.pallas_call(
        functools.partial(norm_kernel, rows, cols),
        name="norms",
        out_shape=jax.ShapeDtypeStruct(squares.shape, f32),
        in_specs=[VMEM],
        out_specs=VMEM,
        scratch_shapes=[pltpu.VMEM((cols - 1,) + squares.shape, f32)] + [pltpu.SemaphoreType.DMA((cols - 1,))] * 2,
        compiler_params=pltpu.CompilerParams(collective_id=ident, has_side_effects=True),
        cost_estimate=cost(1e6, 1 << 20),
    )(squares)


def scatter_kernel(rows, cols, p, gram, high, low, own, gall, ph, pw, q, yr, h, zr, gq, gyr, gh, gzr, send, recv):
    at = Place(rows, cols)
    greet(at.y_peers() + at.z_peers() + at.x_peers() + [at.partner()])
    go = Sender(send, recv)
    blocks, wide = q.shape[0], q.shape[-1]
    rank = p.shape[0]
    size, share = q.shape[3], gq.shape[2]

    def start_y(src, into):
        return [go.start(src.at[:, (at.y + d) % at.flat], into.at[d - 1], at.to_y(d)) for d in range(1, at.flat)]

    def middle(src, into, copies, sums, zinto):
        total = src[:, pl.ds(at.y, 1)][:, 0]
        for d, copy in enumerate(copies):
            copy.wait_recv()
            total = total + into[d]
        sums[...] = total
        return [go.start(sums.at[(at.z + d) % at.deep], zinto.at[d - 1], at.to_z(d)) for d in range(1, at.deep)]

    def last(sums, zinto, copies):
        total = sums[pl.ds(at.z, 1)][0]
        for d, copy in enumerate(copies):
            copy.wait_recv()
            total = total + zinto[d]
        return total

    for i in range(at.deep):
        for j in range(at.flat):
            k = (i * at.flat + j) * share
            gq[i, j] = gram[k : k + share, :]
    gy = start_y(gq, gyr)
    ph[...], pw[...] = split(p[...])
    line = 256

    def multiply(j):
        columns = slice(j * wide, (j + 1) * wide)

        def some(i, carry):
            span = pl.ds(pl.multiple_of(i * line, line), line)
            value = three(nn, (ph[span, :], pw[span, :]), (high[:, columns], low[:, columns]))
            for k in range(line // size):
                chunk = i * (line // size) + k
                q[j, chunk // at.flat, chunk % at.flat] = value[k * size : (k + 1) * size, :]
            return carry

        lax.fori_loop(0, rank // line, some, 0)

    ys, zs = [], []
    gz = gz2 = gy2 = gx = None
    for j in range(blocks):
        multiply(j)
        ys.append(start_y(q.at[j], yr.at[j]))
        if j == 0:
            gz = middle(gq, gyr, gy, gh, gzr)
        if j == 1:
            mine = (at.x, at.core, at.z, at.y)
            gall[mine] = last(gh, gzr, gz)
            gz2 = [go.start(gall.at[mine], gall.at[mine], peer) for peer in at.z_peers()]
    for copy in gz2:
        copy.wait_recv()
    line_at = (at.x, at.core, slice(None), at.y)
    gy2 = [go.start(gall.at[line_at], gall.at[line_at], peer) for peer in at.y_peers()]
    for j in range(blocks):
        zs.append(middle(q.at[j], yr.at[j], ys[j], h.at[j], zr.at[j]))
    for copy in gy2:
        copy.wait_recv()
    gx = [go.start(gall.at[at.x, at.core], gall.at[at.x, at.core], peer) for peer in at.x_peers()]
    for j in range(blocks):
        own[:, j * wide : (j + 1) * wide] = last(h.at[j], zr.at[j], zs[j])
        if j == blocks // 2:
            for copy in gx:
                copy.wait_recv()
            gc = go.start(gall.at[:, at.core], gall.at[:, at.core], at.partner())
    gc.wait_recv()
    go.drain()


def scatter(p, gram, high, low, rows, cols, ident):
    rank, lines = p.shape
    width = high.shape[1]
    blocks = max(1, min(4, width // 256))
    deep = outer_factor(rows)
    flat = rows // deep
    wide, size, share = width // blocks, rank // rows, gram.shape[0] // rows
    xs = cols // CORES
    sends = (blocks + 1) * (deep + flat - 2) + (deep - 1) + (flat - 1) + (xs - 1) + 1
    own, gall = pl.pallas_call(
        functools.partial(scatter_kernel, rows, cols),
        name="scatter",
        out_shape=[jax.ShapeDtypeStruct((size, width), f32), jax.ShapeDtypeStruct((xs, CORES, deep, flat, share, rank), f32)],
        in_specs=[VMEM] * 4,
        out_specs=[VMEM] * 2,
        scratch_shapes=[
            pltpu.VMEM((rank, lines), bf16),
            pltpu.VMEM((rank, lines), bf16),
            pltpu.VMEM((blocks, deep, flat, size, wide), f32),
            pltpu.VMEM((blocks, flat - 1, deep, size, wide), f32),
            pltpu.VMEM((blocks, deep, size, wide), f32),
            pltpu.VMEM((blocks, deep - 1, size, wide), f32),
            pltpu.VMEM((deep, flat, share, rank), f32),
            pltpu.VMEM((flat - 1, deep, share, rank), f32),
            pltpu.VMEM((deep, share, rank), f32),
            pltpu.VMEM((deep - 1, share, rank), f32),
            pltpu.SemaphoreType.DMA((sends,)),
            pltpu.SemaphoreType.DMA((sends,)),
        ],
        compiler_params=pltpu.CompilerParams(collective_id=ident, has_side_effects=True, vmem_limit_bytes=LIMIT),
        cost_estimate=cost(6 * rank * lines * width, 4 * lines * width),
    )(p, gram, high, low)
    return own, gall.reshape(rank, rank)


def shards(rows, cols, momentum, gradient, weight, right_start):
    out_dim, in_dim = momentum.shape[0] * rows, momentum.shape[1] * cols
    rank = right_start.shape[1] * rows
    right = lax.all_gather(right_start.T, "row", axis=0, tiled=True)
    high, low = prepare(momentum, gradient)
    partials, squares = first_product(right, high, low), None
    for iteration in range(ITERS):
        joined = join(partials, squares, rows, cols, 2 * iteration)
        own, gram = scatter(joined[0], joined[1], high, low, rows, cols, 9)
        x = inverse_factor(gram)
        whole = lax.all_gather(own, "row", axis=0, tiled=True)
        if iteration + 1 < ITERS:
            products, squares, partials = solved_product(x, whole, high, low)
    left_high, left_low = left_factor(x, joined[0])
    products, squares = solved_product(x, whole)
    norms = column_norms(squares, rows, cols, 8)
    scale_factor = step_rate * (out_dim * in_dim / rank) ** 0.5
    new_momentum, new_weight = outputs(scale_factor, left_high, left_low, products, norms, momentum, gradient, weight)
    size = rank // rows
    start = lax.axis_index("row") * size
    some = lax.dynamic_slice_in_dim(products, start, size, axis=0)
    norm = lax.dynamic_slice_in_dim(norms[0], start, size, axis=0)
    return new_momentum, new_weight, (some / norm[:, None]).T


def solution(mesh):
    rows, cols = mesh.shape["row"], mesh.shape["col"]
    return jax.shard_map(
        functools.partial(shards, rows, cols),
        mesh=mesh,
        in_specs=(P("row", "col"), P("row", "col"), P("row", "col"), P("col", "row")),
        out_specs=(P("row", "col"), P("row", "col"), P("col", "row")),
        check_vma=False,
    )
```

time: 975 us -> 511 us (0.52)
  waiting for transfers between devices: 613 us -> 142 us
  Pallas kernels: 0 us -> 342 us
  other arithmetic: 188 us -> 1.94 us
  matrix products: 107 us -> 0 us
  blocking collectives: 37.6 us -> 0 us
    pallas_call x0 -> x13, Pallas kernels: none -> 342 us  [the longest x2 139 us: scatter(): pl.pallas_call(functools.partial(scatter_kernel, rows, cols), name='scatt...]
    psum x4 -> x0, waiting for transfers between devices: 260 us -> none  [the longest x2 155 us: shards(): gram_sum = lax.psum(self_gram(left_sum), 'row')]
    another operation x40 -> x0, other arithmetic: 183 us -> none  [the longest x24 99.1 us: solve_rows(): corner = lax.linalg.cholesky(trailing[:size, :size], symmetrize_input=False)]
    reduce_scatter x2 -> x0, waiting for transfers between devices: 178 us -> none  [shards(): lax.psum_scatter(transposed, 'row', scatter_dimension=1, tiled=True)]
    dot_general x34 -> x0, matrix products: 105 us -> none  [the longest x2 24.1 us: shards(): partials = jnp.dot(blended, right_full, precision=wide_mode)]
    all_gather x3, waiting for transfers between devices: 174 us -> 141 us  [the longest x2 76.2 us: shards(): whole = lax.all_gather(own, 'row', axis=0, tiled=True)]
    unnamed x2 -> x0, blocking collectives: 25.4 us -> none
    psum x2 -> x0, blocking collectives: 12.2 us -> none  [shards(): lax.psum(jnp.sum(products * products, axis=0, keepdims=True), 'col')]
  transfers between devices with their start and end apart: 9 -> 3, of which waited for: 9 -> 3; matrix products, arithmetic and copies ran while one was open for 1% -> 0% of each run, Pallas kernels for 0% -> 14%
where the time goes in v1:
time: 511 us; the launch traced here: 502 us
  Pallas kernels  342 us (67%)
  waiting for transfers between devices  142 us (28%)
  between operations  14.2 us (3%)
    pallas_call x2, Pallas kernels, scatter(): pl.pallas_call(functools.partial(scatter_kernel, rows, cols), name='scatt...  139 us
    all_gather x2, waiting for transfers between devices, shards(): whole = lax.all_gather(own, 'row', axis=0, tiled=True)  76.2 us
    pallas_call x2, Pallas kernels, join(): pl.pallas_call(functools.partial(join_kernel, rows, cols, pieces, scaled)...  71.8 us
    all_gather x1, waiting for transfers between devices, shards(): right = lax.all_gather(right_start.T, 'row', axis=0, tiled=True)  65.3 us
    pallas_call x2, Pallas kernels, inverse_factor(): pl.pallas_call(factor_kernel, name='factor', out_shape=jax.ShapeDtypeStru...  57.8 us
    pallas_call x2, Pallas kernels, solved_product(): pl.pallas_call(functools.partial(solved_kernel, high is not None), name='...  24.3 us
    pallas_call x1, Pallas kernels, outputs(): pl.pallas_call(functools.partial(final_kernel, scale_factor), name='outpu...  17.4 us
    pallas_call x1, Pallas kernels, first_product(): pl.pallas_call(first_kernel, name='first', grid=(cols // wide,), in_specs...  11.4 us
  transfers between devices with their start and end apart: 3, of which 3 were waited for; matrix products, arithmetic and copies ran while one was open for 0% of the time, Pallas kernels for 14%

profile of v1, /device:TPU:13, one launch (start us, length us, event | category | flops | bytes accessed | tf_op | source)
XLA Modules:
  0.0 502.1 jit_solution(16105344297814027624)
XLA Ops:
  7.2 0.0 all-gather.4.cloned.1.call-start
  7.2 0.7 all-gather.4.cloned.1.call-update
  7.9 0.0 all-gather.6.cloned.1.call-start
  7.9 7.9 %prepare.1 = (bf16[1024,2048]{1,0:T(8,128)(2,1)}, bf16[1024,2048]{1,0:T(8,128)(2,1)}) custom-call(f32[1024,2048]{1,0:T(8,128)} %m.3, bf16[1024,2048]{1,0:T(8,128)(2,1)} %g.3), custom_call_target="tpu_custom_call" | custom-call | flops 4194304 | bytes 20971520 | tf_op jit(solution)/shard_map/prepare/pallas_call | solution.py:124
  15.8 65.3 %all-gather.4.cloned.1.call-done.r = f32[512,2048]{1,0:T(8,128)} async-done(((f32[64,2048]{1,0:T(8,128)}), f32[512,2048]{1,0:T(8,128)}) %all-gather.4.cloned.1.call-update) | async-done | bytes 4194320 | tf_op jit(solution)/shard_map/all_gather | solution.py:564
  81.1 11.4 %first.1 = f32[512,1024]{1,0:T(8,128)} custom-call(f32[512,2048]{1,0:T(8,128)} %all-gather.4.cloned.1.call-done.r, bf16[1024,2048]{1,0:T(8,128)(2,1)} %get-tuple-element.21.high.refs_0_, bf16[1024,2048]{1,0:T(8,128)(2,1)} %get-tuple-element.22.low.refs_1_), custom_call_target="tpu_custom_call" | custom-call | flops 6442450944 | bytes 8388608 | tf_op jit(solution)/shard_map/first/pallas_call | solution.py:194
  92.5 35.8 %join.2 = (f32[2,4,64,1024]{3,2,1,0:T(8,128)}, f32[128,512]{1,0:T(8,128)}) custom-call(f32[2,4,64,1024]{3,2,1,0:T(8,128)} %bitcast.16), custom_call_target="tpu_custom_call" | custom-call | flops 6000000000 | bytes 6291456 | tf_op jit(solution)/shard_map/join/pallas_call | solution.py:409
  128.3 69.1 %scatter.2 = (f32[64,2048]{1,0:T(8,128)}, f32[2,2,4,2,16,512]{5,4,3,2,1,0:T(8,128)}) custom-call(f32[512,1024]{1,0:T(8,128)} %bitcast.15, f32[128,512]{1,0:T(8,128)} %get-tuple-element.24.gram, bf16[1024,2048]{1,0:T(8,128)(2,1)} %get-tuple-element.21.high.refs_0_, bf16[1024,2048]{1,0:T(8,128)(2,1)} %get-tuple-element.22.low.refs_1_), custom_call_target="tpu_custom_call" | custom-call | flops 6442450944 | bytes 8388608 | tf_op jit(solution)/shard_map/scatter/pallas_call | solution.py:535
  197.4 0.0 all-gather.6.cloned.1.call-update
  197.4 0.5 all-gather.8.cloned.1.call-start
  198.0 28.9 %factor.2.x = f32[512,512]{1,0:T(8,128)} custom-call(f32[512,512]{1,0:T(8,128)} %bitcast.18), custom_call_target="tpu_custom_call" | custom-call | flops 20000000000 | bytes 2097152 | tf_op jit(solution)/shard_map/factor/pallas_call | solution.py:104
  226.8 40.6 %all-gather.6.cloned.1.call-done.q = f32[512,2048]{1,0:T(8,128)} async-done(((f32[64,2048]{1,0:T(8,128)}), f32[512,2048]{1,0:T(8,128)}) %all-gather.6.cloned.1.call-update) | async-done | bytes 4194320 | tf_op jit(solution)/shard_map/all_gather | solution.py:571
  267.4 16.7 %solved.2 = (f32[512,2048]{1,0:T(8,128)}, f32[8,512]{1,0:T(8,128)}, f32[512,1024]{1,0:T(8,128)}) custom-call(f32[512,512]{1,0:T(8,128)} %factor.2.x, f32[512,2048]{1,0:T(8,128)} %all-gather.6.cloned.1.call-done.q, bf16[1024,2048]{1,0:T(8,128)(2,1)} %get-tuple-element.21.high.refs_0_, bf16[1024,2048]{1,0:T(8,128)(2,1)} %get-tuple-element.22.low.refs_1_), custom_call_target="tpu_custom_call" | custom-call | flops 6442450944 | bytes 8388608 | tf_op jit(solution)/shard_map/solved/pallas_call | solution.py:220
  284.2 36.0 %join.3 = (f32[2,4,64,1024]{3,2,1,0:T(8,128)}, f32[128,512]{1,0:T(8,128)}, f32[8,512]{1,0:T(8,128)}) custom-call(f32[2,4,64,1024]{3,2,1,0:T(8,128)} %bitcast.14, f32[8,512]{1,0:T(8,128)} %get-tuple-element.28.refs_1_), custom_call_target="tpu_custom_call" | custom-call | flops 6000000000 | bytes 6291456 | tf_op jit(solution)/shard_map/join/pallas_call | solution.py:409
  320.1 70.1 %scatter.3 = (f32[64,2048]{1,0:T(8,128)}, f32[2,2,4,2,16,512]{5,4,3,2,1,0:T(8,128)}) custom-call(f32[512,1024]{1,0:T(8,128)} %bitcast.12, f32[128,512]{1,0:T(8,128)} %get-tuple-element.30.gram, bf16[1024,2048]{1,0:T(8,128)(2,1)} %get-tuple-element.21.high.refs_0_, bf16[1024,2048]{1,0:T(8,128)(2,1)} %get-tuple-element.22.low.refs_1_), custom_call_target="tpu_custom_call" | custom-call | flops 6442450944 | bytes 8388608 | tf_op jit(solution)/shard_map/scatter/pallas_call | solution.py:535
  390.3 0.0 all-gather.8.cloned.1.call-update
  390.3 28.9 %factor.3.x = f32[512,512]{1,0:T(8,128)} custom-call(f32[512,512]{1,0:T(8,128)} %bitcast.17), custom_call_target="tpu_custom_call" | custom-call | flops 20000000000 | bytes 2097152 | tf_op jit(solution)/shard_map/factor/pallas_call | solution.py:104
  419.2 5.5 %left.1 = (bf16[1024,512]{1,0:T(8,128)(2,1)}, bf16[1024,512]{1,0:T(8,128)(2,1)}) custom-call(f32[512,512]{1,0:T(8,128)} %factor.3.x, f32[512,1024]{1,0:T(8,128)} %bitcast.13), custom_call_target="tpu_custom_call" | custom-call | flops 1610612736 | bytes 4194304 | tf_op jit(solution)/shard_map/left/pallas_call | solution.py:243
  424.7 35.6 %all-gather.8.cloned.1.call-done.q = f32[512,2048]{1,0:T(8,128)} async-done(((f32[64,2048]{1,0:T(8,128)}), f32[512,2048]{1,0:T(8,128)}) %all-gather.8.cloned.1.call-update) | async-done | bytes 4194320 | tf_op jit(solution)/shard_map/all_gather | solution.py:571
  460.3 7.6 %solved.3 = (f32[512,2048]{1,0:T(8,128)}, f32[8,512]{1,0:T(8,128)}) custom-call(f32[512,512]{1,0:T(8,128)} %factor.3.x, f32[512,2048]{1,0:T(8,128)} %all-gather.8.cloned.1.call-done.q), custom_call_target="tpu_custom_call" | custom-call | flops 6442450944 | bytes 8388608 | tf_op jit(solution)/shard_map/solved/pallas_call | solution.py:220
  467.9 7.1 %norms.1 = f32[8,512]{1,0:T(8,128)} custom-call(f32[8,512]{1,0:T(8,128)} %get-tuple-element.36.sq), custom_call_target="tpu_custom_call" | custom-call | flops 1000000 | bytes 1048576 | tf_op jit(solution)/shard_map/norms/pallas_call | solution.py:437
  475.0 0.7 slice.3
  475.7 0.1 dynamic-slice_bitcast_fusion
  475.8 1.9 divide_bitcast_fusion
  477.7 17.4 %outputs.1 = (f32[1024,2048]{1,0:T(8,128)}, bf16[1024,2048]{1,0:T(8,128)(2,1)}) custom-call(bf16[1024,512]{1,0:T(8,128)(2,1)} %get-tuple-element.32.high, bf16[1024,512]{1,0:T(8,128)(2,1)} %get-tuple-element.33.low, f32[512,2048]{1,0:T(8,128)} %get-tuple-element.35.q, f32[8,512]{1,0:T(8,128)} %norms.1, f32[1024,2048]{1,0:T(8,128)} %m.3, ...), custom_call_target="tpu_custom_call" | custom-call | flops 8589934592 | bytes 29360128 | tf_op jit(solution)/shard_map/outputs/pallas_call | solution.py:272
Async XLA Ops:
  7.2 73.9 %all-gather.4.cloned.1.call-start = ((), (), s32[]{:S(2)}) async-start(), calls=%async_computation | async-start | bytes 4718592 | tf_op jit(solution)/shard_map/all_gather | solution.py:564
  7.9 259.5 %all-gather.6.cloned.1.call-start = ((), (), s32[]{:S(2)}) async-start(), calls=%async_computation.1 | async-start | bytes 4718592 | tf_op jit(solution)/shard_map/all_gather | solution.py:571
  197.4 262.8 %all-gather.8.cloned.1.call-start = ((), (), s32[]{:S(2)}) async-start(), calls=%async_computation.2 | async-start | bytes 4718592 | tf_op jit(solution)/shard_map/all_gather | solution.py:571
Sparse Core Ops, SparseCore 0:
  10.1 70.9 all-gather.3
  197.6 69.8 all-gather.5
  390.4 69.8 all-gather.7

commit v2 on v0

v2 whole, which is shorter than its diff:
```python
import functools

import jax
import jax.numpy as jnp
from jax import lax
from jax.experimental import pallas as pl
from jax.experimental.pallas import tpu as pltpu
from jax.sharding import PartitionSpec as P

ITERS = 2
CORES = 2
momentum_decay = 0.9
step_rate = 0.1
epsilon = 1e-06
exact = lax.Precision.HIGHEST
f32, bf16 = jnp.float32, jnp.bfloat16
VMEM = pl.BlockSpec(memory_space=pltpu.VMEM)
MESH = pl.DeviceIdType.MESH
LIMIT = 56 << 20


def nt(a, b, precision=None):
    return lax.dot_general(a, b, (((1,), (1,)), ((), ())), precision=precision, preferred_element_type=f32)


def nn(a, b, precision=None):
    return lax.dot_general(a, b, (((1,), (0,)), ((), ())), precision=precision, preferred_element_type=f32)


def split(x):
    high = x.astype(bf16)
    return high, (x - high.astype(f32)).astype(bf16)


def three(dot, a, b):
    return (dot(a[1], b[0]) + dot(a[0], b[1])) + dot(a[0], b[0])


def outer_factor(n):
    d = 1
    while d * d < n or n % d:
        d += 1
    return d


def cost(flops, moved):
    return pl.CostEstimate(flops=int(flops), bytes_accessed=int(moved), transcendentals=0)


def eye(n):
    return (lax.broadcasted_iota(jnp.int32, (n, n), 0) == lax.broadcasted_iota(jnp.int32, (n, n), 1)).astype(f32)


def eliminate(a, w):
    size = a.shape[0]
    shape = (8, size)
    sub = lax.broadcasted_iota(jnp.int32, shape, 0)
    w[...] = eye(size)
    for at in range(0, size, 8):
        slab, inv_rows = a[at : at + 8, :], w[at : at + 8, :]
        cols = [jnp.broadcast_to(slab[:, at + i : at + i + 1], shape) for i in range(8)]
        scale = jnp.zeros(shape, f32)
        for i in range(8):
            pivot = jnp.broadcast_to(cols[i][i : i + 1, :], shape)
            scale = jnp.where(sub == i, lax.rsqrt(pivot), scale)
            if i < 7:
                m = jnp.where(sub > i, cols[i] / pivot, 0.0)
                for k in range(i + 1, 8):
                    cols[k] = cols[k] - m * jnp.broadcast_to(cols[k][i : i + 1, :], shape)
                slab = slab - m * jnp.broadcast_to(slab[i : i + 1, :], shape)
                inv_rows = inv_rows - m * jnp.broadcast_to(inv_rows[i : i + 1, :], shape)
        upper, inv_rows = slab * scale, inv_rows * scale
        w[at : at + 8, :] = inv_rows
        lower = upper.T
        for k in range(at + 8, size, 8):
            rows, inv = a[k : k + 8, :], w[k : k + 8, :]
            for i in range(8):
                factor = jnp.broadcast_to(lower[k : k + 8, i : i + 1], shape)
                rows = rows - factor * jnp.broadcast_to(upper[i : i + 1, :], shape)
                inv = inv - factor * jnp.broadcast_to(inv_rows[i : i + 1, :], shape)
            a[k : k + 8, :] = rows
            w[k : k + 8, :] = inv


def factor_step(step, work, x, a, w):
    rank, block = work.shape[0], a.shape[0]
    span = pl.ds(pl.multiple_of(step * block, block), block)
    a[...] = work[span, span]
    eliminate(a, w)
    inverse = w[...]
    below = lax.broadcasted_iota(jnp.int32, (rank, block), 0) >= (step + 1) * block
    panel = jnp.where(below, nt(work[:, span], inverse, exact), 0.0)
    solved = nn(inverse, x[span, :], exact)
    x[...] = x[...] - nn(panel, solved, exact)
    x[span, :] = solved
    work[...] = work[...] - nt(panel, panel, exact)


def row_sums(total):
    rank = total.shape[0]
    column = jnp.sum(total, axis=1, keepdims=True)
    return jnp.broadcast_to(column, (rank, 128)).T[:8, :]


def final_kernel(scale_factor, high, low, q, norms, m, g, weight, new_m, new_w):
    rank = q.shape[0]
    column = jnp.broadcast_to(norms[0:1, :], (128, rank)).T[:, 0:1]
    s = q[...]
    left = (high[...], low[...])
    blended = m[...] + g[...].astype(f32)
    new_m[...] = blended - (1.0 - momentum_decay) * nn(left[0], s.astype(bf16))
    update = three(nn, left, split(s / column))
    new_w[...] = (weight[...].astype(f32) - scale_factor * update).astype(bf16)


def outputs(scale_factor, high, low, q, norms, momentum, gradient, weight):
    rank, cols = q.shape
    rows = high.shape[0]
    wide = min(256, cols)
    side = pl.BlockSpec((rows, rank), lambda j: (0, 0))
    block = pl.BlockSpec((rows, wide), lambda j: (0, j))
    return pl.pallas_call(
        functools.partial(final_kernel, scale_factor),
        name="outputs",
        grid=(cols // wide,),
        in_specs=[side, side, pl.BlockSpec((rank, wide), lambda j: (0, j)), pl.BlockSpec((8, rank), lambda j: (0, 0)), block, block, block],
        out_specs=[block, block],
        out_shape=[jax.ShapeDtypeStruct((rows, cols), f32), jax.ShapeDtypeStruct((rows, cols), bf16)],
        compiler_params=pltpu.CompilerParams(vmem_limit_bytes=LIMIT),
        cost_estimate=cost(8 * rank * rows * cols, 14 * rows * cols),
    )(high, low, q, norms, momentum, gradient, weight)


class Place:
    def __init__(self, rows, cols):
        self.deep = outer_factor(rows)
        self.flat = rows // self.deep
        self.wide = cols // CORES
        self.row, self.col = lax.axis_index("row"), lax.axis_index("col")
        self.z, self.y = self.row // self.flat, self.row % self.flat
        self.x, self.core = self.col // CORES, self.col % CORES

    def to_y(self, d):
        return (self.z * self.flat + (self.y + d) % self.flat, self.col)

    def to_z(self, d):
        return (((self.z + d) % self.deep) * self.flat + self.y, self.col)

    def to_x(self, d):
        return (self.row, ((self.x + d) % self.wide) * CORES + self.core)

    def partner(self):
        return (self.row, self.x * CORES + 1 - self.core)

    def y_peers(self):
        return [self.to_y(d) for d in range(1, self.flat)]

    def z_peers(self):
        return [self.to_z(d) for d in range(1, self.deep)]

    def x_peers(self):
        return [self.to_x(d) for d in range(1, self.wide)]


def greet(peers):
    barrier = pltpu.get_barrier_semaphore()
    for peer in peers:
        pl.semaphore_signal(barrier, inc=1, device_id=peer, device_id_type=MESH)
    pl.semaphore_wait(barrier, len(peers))


class Sender:
    def __init__(self, send, recv):
        self.send, self.recv, self.copies = send, recv, []

    def start(self, src, dst, peer):
        at = len(self.copies)
        copy = pltpu.make_async_remote_copy(
            src_ref=src, dst_ref=dst, send_sem=self.send.at[at], recv_sem=self.recv.at[at], device_id=peer, device_id_type=MESH
        )
        copy.start()
        self.copies.append(copy)
        return copy

    def drain(self):
        for copy in self.copies:
            copy.wait_send()


PIECES = 4


def iterate_kernel(rows, cols, units, blocks, mode, *refs):
    if mode == 0:
        own, m, g, high, low, out, chunk, gall = refs[:8]
        refs = refs[8:]
    else:
        own, gram, high, low, out, chunk, gall = refs[:7]
        x, xh, xl, a, w, work, total, sq, sq_in, ss, sr = refs[7:18]
        refs = refs[18:]
    whole, part, half, near, far, gram_own, ph, pw, q, qy, h, hz, gq, gyr, gh, gzr, zs, zr, ys, yr = refs[:20]
    join_s, join_r, far_s, far_r, back_s, back_r, qy_s, qy_r, hz_s, hz_r, send, recv = refs[20:]
    at = Place(rows, cols)
    peers = at.y_peers() + at.z_peers()
    col_peers = [(at.row, (at.col + d) % cols) for d in range(1, cols)]
    greet(peers + (col_peers if mode else at.x_peers() + [at.partner()]))
    size, wide = whole.shape[3], whole.shape[4]
    rank, middle_rank = size * rows * (2 if mode else 1), part.shape[1] * part.shape[2] * part.shape[3]
    lines = part.shape[-1]
    step_lanes = units // 2

    def remote(src, dst, send_sem, recv_sem, peer):
        return pltpu.make_async_remote_copy(
            src_ref=src, dst_ref=dst, send_sem=send_sem, recv_sem=recv_sem, device_id=peer, device_id_type=MESH
        )

    def spread(at_index, count):
        if isinstance(at_index, int):
            return slice(at_index * count, (at_index + 1) * count)
        return pl.ds(pl.multiple_of(at_index * count, count), count)

    def loop(start, count, body):
        lax.fori_loop(start, count, lambda j, c: (body(j), c)[1], 0)

    def lanes(u):
        return spread(u % step_lanes, wide) if mode else spread(u, wide)

    def source(u):
        return own.at[u // step_lanes, :, lanes(u)] if mode else own.at[:, lanes(u)]

    def z_copy(u, d):
        return remote(source(u), whole.at[u, at.z, at.y], zs.at[u, d - 1], zr.at[u, d - 1], at.to_z(d))

    def y_copy(u, e, d):
        piece = whole.at[u, (at.z - d + at.deep) % at.deep, at.y]
        return remote(source(u) if d == 0 else piece, piece, ys.at[u, e - 1, d], yr.at[u, e - 1, d], at.to_y(e))

    for u in range(units):
        for d in range(1, at.deep):
            z_copy(u, d).start()
        for e in range(1, at.flat):
            y_copy(u, e, 0).start()
    for u in range(units):
        whole[u, at.z, at.y] = own[u // step_lanes, :, lanes(u)] if mode else own[:, lanes(u)]

    def forward(u):
        for d in range(1, at.deep):
            z_copy(u, d).wait_recv()
            for e in range(1, at.flat):
                y_copy(u, e, d).start()

    def arrived(u):
        for e in range(1, at.flat):
            for d in range(at.deep):
                y_copy(u, e, d).wait_recv()

    mine, other = at.core, 1 - at.core

    def near_copy(r, k):
        return remote(part.at[r, other, k], near.at[r, k], join_s.at[r, k], join_r.at[r, k], at.partner())

    def far_copy(r, k, d):
        return remote(half.at[r, k], far.at[r, d - 1, k], far_s.at[r, k, d - 1], far_r.at[r, k, d - 1], at.to_x(d))

    def back_copy(r, k):
        return remote(out.at[r, mine, k], out.at[r, mine, k], back_s.at[r, k], back_r.at[r, k], at.partner())

    def sq_copy(r, d):
        return remote(sq.at[r], sq_in.at[r, d - 1], ss.at[r, d - 1], sr.at[r, d - 1], (at.row, (at.col + d) % cols))

    def join_begin(r):
        if mode:
            sq[r] = row_sums(total[r])
            for d in range(1, cols):
                sq_copy(r, d).start()
        for k in range(PIECES):
            near_copy(r, k).start()
        for k in range(PIECES):
            near_copy(r, k).wait_recv()
            half[r, k] = part[r, mine, k] + near[r, k]
            for d in range(1, at.wide):
                far_copy(r, k, d).start()

    def join_end(r):
        if mode:
            value = sq[r]
            for d in range(1, cols):
                sq_copy(r, d).wait_recv()
                value = value + sq_in[r, d - 1]
            norm = jnp.sqrt(value + epsilon)
            column = jnp.broadcast_to(norm[0:1, :], (128, middle_rank)).T[:, 0:1]
            count = middle_rank // (CORES * PIECES)
        for k in range(PIECES):
            value = half[r, k]
            for d in range(1, at.wide):
                far_copy(r, k, d).wait_recv()
                value = value + far[r, d - 1, k]
            if mode:
                first = column[k * count : (k + 1) * count]
                value = value / jnp.where(mine == 0, first, column[(PIECES + k) * count : (PIECES + k + 1) * count])
            out[r, mine, k] = value
            back_copy(r, k).start()
        for k in range(PIECES):
            back_copy(r, k).wait_recv()

    q_size, q_wide = q.shape[4], q.shape[5]

    def qy_copy(r, j, e):
        return remote(q.at[r, j, :, (at.y + e) % at.flat], qy.at[r, j, e - 1], qy_s.at[r, j, e - 1], qy_r.at[r, j, e - 1], at.to_y(e))

    def hz_copy(r, j, d):
        return remote(h.at[r, j, (at.z + d) % at.deep], hz.at[r, j, d - 1], hz_s.at[r, j, d - 1], hz_r.at[r, j, d - 1], at.to_z(d))

    def multiply(r):
        ph[...], pw[...] = split(out[r].reshape(middle_rank, lines))

        def turn(j):
            columns = spread(j, q_wide)
            value = three(nn, (ph[...], pw[...]), (high[:, columns], low[:, columns]))
            q[r, j] = value.reshape(at.deep, at.flat, q_size, q_wide)
            for e in range(1, at.flat):
                qy_copy(r, j, e).start()

        loop(0, blocks, turn)

    def middle(r, j):
        value = q[r, j, :, pl.ds(at.y, 1)][:, 0]
        for e in range(1, at.flat):
            qy_copy(r, j, e).wait_recv()
            value = value + qy[r, j, e - 1]
        h[r, j] = value
        for d in range(1, at.deep):
            hz_copy(r, j, d).start()

    def last(r, j):
        value = h[r, j, pl.ds(at.z, 1)][0]
        for d in range(1, at.deep):
            hz_copy(r, j, d).wait_recv()
            value = value + hz[r, j, d - 1]
        chunk[r, :, spread(j, q_wide)] = value

    def add(r, u, value):
        product = three(nt, split(value), (high[:, lanes(u)], low[:, lanes(u)]))

        @pl.when(lanes_at(u) == 0)
        def _():
            if mode:
                part[r] = product.reshape(part.shape[1:])
            else:
                part[...] = product.reshape(part.shape)

        @pl.when(lanes_at(u) > 0)
        def _():
            if mode:
                part[r] = part[r] + product.reshape(part.shape[1:])
            else:
                part[...] = part[...] + product.reshape(part.shape)

    def lanes_at(u):
        return u % step_lanes if mode else u

    if mode == 0:
        count = m.shape[0] // units

        def divide(j):
            span = spread(j, count)
            high[span, :], low[span, :] = split(m[span, :] + g[span, :].astype(f32))

        loop(0, units, divide)
        forward(0)

        def turn(u):
            forward(u + 1)
            arrived(u)
            add(0, u, whole[u].reshape(rank, wide))

        loop(0, units - 1, turn)
        arrived(units - 1)
        add(0, jnp.int32(units - 1), whole[units - 1].reshape(rank, wide))
        join_begin(0)
        join_begin(1)
    else:
        work[...] = gram[...]
        x[...] = eye(rank)

        def step(u):
            factor_step(u, work, x, a, w)

            @pl.when(u > 0)
            def _():
                forward(u - 1)

        loop(0, units, step)
        xh[...], xl[...] = split(x[...])
        total[...] = jnp.zeros_like(total)

        def solve(r, u):
            arrived(u)
            span = slice(r * middle_rank, (r + 1) * middle_rank)
            s = jnp.zeros((middle_rank, wide), f32)
            for k in range(r + 1):
                columns = slice(k * middle_rank, (k + 1) * middle_rank)
                value = whole[u - (r - k) * step_lanes].reshape(middle_rank, wide)
                s = s + three(nn, (xh[span, columns], xl[span, columns]), split(value))
            sums = total[r]
            for k in range(0, wide, 128):
                sums = sums + s[:, k : k + 128] * s[:, k : k + 128]
            total[r] = sums
            add(r, u, s)

        loop(0, step_lanes, lambda u: solve(0, u))
        join_begin(0)
        forward(units - 1)
        loop(step_lanes, units, lambda u: solve(1, u))
        join_begin(1)

    join_end(0)
    multiply(0)
    middle(0, 0)
    join_end(1)
    own_rows = gram_own.shape[0]
    shares = PIECES * part.shape[3] // own_rows
    place = at.col // shares
    take = own_rows // part.shape[3]
    picked = out[place // CORES, place % CORES, pl.ds((at.col % shares) * take, take)].reshape(own_rows, lines)
    gram_own[...] = nt(picked, out[...].reshape(2 * middle_rank, lines), exact)
    share = gq.shape[2]
    for i in range(at.deep):
        for j in range(at.flat):
            k = (i * at.flat + j) * share
            gq[i, j] = gram_own[k : k + share, :]
    go = Sender(send, recv)
    gy = [go.start(gq.at[:, (at.y + e) % at.flat], gyr.at[e - 1], at.to_y(e)) for e in range(1, at.flat)]
    multiply(1)
    loop(1, blocks, lambda j: middle(0, j))
    value = gq[:, pl.ds(at.y, 1)][:, 0]
    for d, copy in enumerate(gy):
        copy.wait_recv()
        value = value + gyr[d]
    gh[...] = value
    gz = [go.start(gh.at[(at.z + d) % at.deep], gzr.at[d - 1], at.to_z(d)) for d in range(1, at.deep)]
    loop(0, blocks, lambda j: last(0, j))
    middle(1, 0)
    value = gh[pl.ds(at.z, 1)][0]
    for d, copy in enumerate(gz):
        copy.wait_recv()
        value = value + gzr[d]
    here = (at.x, at.core, at.z, at.y)
    gall[here] = value
    gz = [go.start(gall.at[here], gall.at[here], peer) for peer in at.z_peers()]
    loop(1, (blocks + 1) // 2, lambda j: middle(1, j))
    for copy in gz:
        copy.wait_recv()
    line_at = (at.x, at.core, slice(None), at.y)
    gy = [go.start(gall.at[line_at], gall.at[line_at], peer) for peer in at.y_peers()]
    loop((blocks + 1) // 2, blocks, lambda j: middle(1, j))
    for copy in gy:
        copy.wait_recv()
    gx = [go.start(gall.at[at.x, at.core], gall.at[at.x, at.core], peer) for peer in at.x_peers()]
    loop(0, blocks - 1, lambda j: last(1, j))
    for copy in gx:
        copy.wait_recv()
    gc = go.start(gall.at[:, at.core], gall.at[:, at.core], at.partner())
    last(1, blocks - 1)
    gc.wait_recv()
    go.drain()

    def finish(u):
        for d in range(1, at.deep):
            z_copy(u, d).wait_send()
        for e in range(1, at.flat):
            for d in range(at.deep):
                y_copy(u, e, d).wait_send()

    loop(0, units, finish)
    for r in range(2):
        for k in range(PIECES):
            near_copy(r, k).wait_send()
            back_copy(r, k).wait_send()
            for d in range(1, at.wide):
                far_copy(r, k, d).wait_send()
        if mode:
            for d in range(1, cols):
                sq_copy(r, d).wait_send()

        def sent(j):
            for e in range(1, at.flat):
                qy_copy(r, j, e).wait_send()
            for d in range(1, at.deep):
                hz_copy(r, j, d).wait_send()

        loop(0, blocks, sent)


def iterate(mode, rows, cols, ident, own, *args):
    width = own.shape[-1]
    lines = args[-1].shape[0]
    rank = own.size // width * rows
    deep = outer_factor(rows)
    flat = rows // deep
    xs = cols // CORES
    units = 4
    size = rank // rows // (2 if mode else 1)
    wide = width // units * (2 if mode else 1)
    blocks = max(1, min(4, width // 256))
    half_rank, q_wide, q_size = rank // 2, width // blocks, rank // rows // 2
    piece = half_rank // (CORES * PIECES)
    share = rank // cols // rows
    dma = pltpu.SemaphoreType.DMA
    out_shape = [
        jax.ShapeDtypeStruct((2, CORES, PIECES, piece, lines), f32),
        jax.ShapeDtypeStruct((2, q_size, width), f32),
        jax.ShapeDtypeStruct((xs, CORES, deep, flat, share, rank), f32),
    ]
    scratch = []
    if mode == 0:
        out_shape = [jax.ShapeDtypeStruct((lines, width), bf16)] * 2 + out_shape
    else:
        block = rank // units
        scratch = [pltpu.VMEM((rank, rank), f32)] + [pltpu.VMEM((rank, rank), bf16)] * 2
        scratch += [pltpu.VMEM((block, block), f32)] * 2 + [pltpu.VMEM((rank, rank), f32), pltpu.VMEM((2, half_rank, 128), f32)]
        scratch += [pltpu.VMEM((2, 8, half_rank), f32), pltpu.VMEM((2, cols - 1, 8, half_rank), f32)]
        scratch += [dma((2, cols - 1))] * 2
    scratch += [
        pltpu.VMEM((units, deep, flat, size, wide), f32),
        pltpu.VMEM((2, CORES, PIECES, piece, lines), f32),
        pltpu.VMEM((2, PIECES, piece, lines), f32),
        pltpu.VMEM((2, PIECES, piece, lines), f32),
        pltpu.VMEM((2, xs - 1, PIECES, piece, lines), f32),
        pltpu.VMEM((rank // cols, rank), f32),
        pltpu.VMEM((half_rank, lines), bf16),
        pltpu.VMEM((half_rank, lines), bf16),
        pltpu.VMEM((2, blocks, deep, flat, q_size, q_wide), f32),
        pltpu.VMEM((2, blocks, flat - 1, deep, q_size, q_wide), f32),
        pltpu.VMEM((2, blocks, deep, q_size, q_wide), f32),
        pltpu.VMEM((2, blocks, deep - 1, q_size, q_wide), f32),
        pltpu.VMEM((deep, flat, share, rank), f32),
        pltpu.VMEM((flat - 1, deep, share, rank), f32),
        pltpu.VMEM((deep, share, rank), f32),
        pltpu.VMEM((deep - 1, share, rank), f32),
    ]
    scratch += [dma((units, deep - 1))] * 2 + [dma((units, flat - 1, deep))] * 2
    scratch += [dma((2, PIECES))] * 2 + [dma((2, PIECES, xs - 1))] * 2 + [dma((2, PIECES))] * 2
    scratch += [dma((2, blocks, flat - 1))] * 2 + [dma((2, blocks, deep - 1))] * 2
    scratch += [dma((2 * (deep - 1) + 2 * (flat - 1) + xs,))] * 2
    res = pl.pallas_call(
        functools.partial(iterate_kernel, rows, cols, units, blocks, mode),
        name="iterate",
        out_shape=out_shape,
        in_specs=[VMEM] * (1 + len(args)),
        out_specs=[VMEM] * len(out_shape),
        scratch_shapes=scratch,
        compiler_params=pltpu.CompilerParams(collective_id=ident, has_side_effects=True, vmem_limit_bytes=LIMIT),
        cost_estimate=cost(6e10, 24 << 20),
    )(own, *args)
    joined, chunk, gall = res[-3:]
    return list(res[:-3]) + [joined.reshape(rank, lines), chunk, gall.reshape(rank, rank)]


def gather_kernel(rows, cols, blocks, *refs):
    own, gram, p, solved, norms, left_high, left_low = refs[:7]
    whole, x, xh, xl, a, w, work, total, sq, sq_in, ss, sr, zs, zr, ys, yr = refs[7:]
    at = Place(rows, cols)
    col_peers = [(at.row, (at.col + d) % cols) for d in range(1, cols)]
    greet(at.y_peers() + at.z_peers() + col_peers)
    wide, size = whole.shape[-1], own.shape[0]
    rank = size * rows

    def lanes(j):
        if isinstance(j, int):
            return slice(j * wide, (j + 1) * wide)
        return pl.ds(pl.multiple_of(j * wide, wide), wide)

    def z_copy(j, d):
        return pltpu.make_async_remote_copy(
            src_ref=own.at[:, lanes(j)],
            dst_ref=whole.at[j, at.z, at.y],
            send_sem=zs.at[j, d - 1],
            recv_sem=zr.at[j, d - 1],
            device_id=at.to_z(d),
            device_id_type=MESH,
        )

    def y_copy(j, e, d):
        chunk = whole.at[j, (at.z - d + at.deep) % at.deep, at.y]
        return pltpu.make_async_remote_copy(
            src_ref=own.at[:, lanes(j)] if d == 0 else chunk,
            dst_ref=chunk,
            send_sem=ys.at[j, e - 1, d],
            recv_sem=yr.at[j, e - 1, d],
            device_id=at.to_y(e),
            device_id_type=MESH,
        )

    for j in range(blocks):
        for d in range(1, at.deep):
            z_copy(j, d).start()
        for e in range(1, at.flat):
            y_copy(j, e, 0).start()
    for j in range(blocks):
        whole[j, at.z, at.y] = own[:, lanes(j)]

    def forward(j):
        for d in range(1, at.deep):
            z_copy(j, d).wait_recv()
            for e in range(1, at.flat):
                y_copy(j, e, d).start()

    def block(j):
        for e in range(1, at.flat):
            for d in range(at.deep):
                y_copy(j, e, d).wait_recv()
        return jnp.swapaxes(whole[j].reshape(rows, 2, size // 2, wide), 0, 1).reshape(rank, wide)

    def loop(count, body):
        lax.fori_loop(0, count, lambda j, c: (body(j), c)[1], 0)

    work[...] = gram[...]
    x[...] = eye(rank)

    def step(j):
        factor_step(j, work, x, a, w)

        @pl.when(j > 0)
        def _():
            forward(j - 1)

    loop(blocks, step)
    xh[...], xl[...] = split(x[...])
    lines = min(256, p.shape[1])

    def left(i):
        span = pl.ds(pl.multiple_of(i * lines, lines), lines)
        value = three(nn, (xh[...], xl[...]), split(p[:, span])).T
        left_high[span, :], left_low[span, :] = split(value)

    loop(p.shape[1] // lines, left)
    total[...] = jnp.zeros_like(total)

    def turn(j):
        s = three(nn, (xh[...], xl[...]), split(block(j)))
        sums = total[...]
        for k in range(0, wide, 128):
            sums = sums + s[:, k : k + 128] * s[:, k : k + 128]
        total[...] = sums
        solved[:, lanes(j)] = s

        @pl.when(j == min(1, blocks - 1))
        def _():
            forward(blocks - 1)

    if blocks == 1:
        forward(0)
    loop(blocks, turn)
    sq[...] = row_sums(total[...])
    go = Sender(ss, sr)
    copies = [go.start(sq, sq_in.at[d], peer) for d, peer in enumerate(col_peers)]
    value = sq[...]
    for d, copy in enumerate(copies):
        copy.wait_recv()
        value = value + sq_in[d]
    norms[...] = jnp.sqrt(value + epsilon)
    go.drain()
    for j in range(blocks):
        for d in range(1, at.deep):
            z_copy(j, d).wait_send()
        for e in range(1, at.flat):
            for d in range(at.deep):
                y_copy(j, e, d).wait_send()


def gather(rows, cols, ident, own, gram, p):
    size, width = own.shape
    rank, lines = p.shape
    blocks = max(1, min(4, width // 256, rank // 128))
    deep = outer_factor(rows)
    flat = rows // deep
    block = rank // blocks
    dma = pltpu.SemaphoreType.DMA
    out_shape = [jax.ShapeDtypeStruct((rank, width), f32), jax.ShapeDtypeStruct((8, rank), f32)]
    out_shape += [jax.ShapeDtypeStruct((lines, rank), bf16)] * 2
    scratch = [pltpu.VMEM((blocks, deep, flat, size, width // blocks), f32)]
    scratch += [pltpu.VMEM((rank, rank), f32)] + [pltpu.VMEM((rank, rank), bf16)] * 2
    scratch += [pltpu.VMEM((block, block), f32)] * 2 + [pltpu.VMEM((rank, rank), f32), pltpu.VMEM((rank, 128), f32)]
    scratch += [pltpu.VMEM((8, rank), f32), pltpu.VMEM((cols - 1, 8, rank), f32)] + [dma((cols - 1,))] * 2
    scratch += [dma((blocks, deep - 1))] * 2 + [dma((blocks, flat - 1, deep))] * 2
    return pl.pallas_call(
        functools.partial(gather_kernel, rows, cols, blocks),
        name="gather",
        out_shape=out_shape,
        in_specs=[VMEM] * 3,
        out_specs=[VMEM] * len(out_shape),
        scratch_shapes=scratch,
        compiler_params=pltpu.CompilerParams(collective_id=ident, has_side_effects=True, vmem_limit_bytes=LIMIT),
        cost_estimate=cost(3e10, 16 << 20),
    )(own, gram, p)


def shards(rows, cols, momentum, gradient, weight, right_start):
    out_dim, in_dim = momentum.shape[0] * rows, momentum.shape[1] * cols
    rank = right_start.shape[1] * rows
    high, low, joined, own, gram = iterate(0, rows, cols, 0, right_start.T, momentum, gradient)
    for iteration in range(1, ITERS):
        joined, own, gram = iterate(1, rows, cols, 1, own, gram, high, low)
    own = own.reshape(rank // rows, own.shape[-1])
    products, norms, left_high, left_low = gather(rows, cols, 2, own, gram, joined)
    scale_factor = step_rate * (out_dim * in_dim / rank) ** 0.5
    new_momentum, new_weight = outputs(scale_factor, left_high, left_low, products, norms, momentum, gradient, weight)
    size = rank // rows
    start = lax.axis_index("row") * size
    some = lax.dynamic_slice_in_dim(products, start, size, axis=0)
    norm = lax.dynamic_slice_in_dim(norms[0], start, size, axis=0)
    return new_momentum, new_weight, (some / norm[:, None]).T


def solution(mesh):
    rows, cols = mesh.shape["row"], mesh.shape["col"]
    return jax.shard_map(
        functools.partial(shards, rows, cols),
        mesh=mesh,
        in_specs=(P("row", "col"), P("row", "col"), P("row", "col"), P("col", "row")),
        out_specs=(P("row", "col"), P("row", "col"), P("col", "row")),
        check_vma=False,
    )
```

time: 975 us -> 389 us (0.40); the launches traced: 965 us -> 388 us
  waiting for transfers between devices: 613 us -> 0 us
  Pallas kernels: 0 us -> 385 us
  other arithmetic: 188 us -> 1.94 us
  matrix products: 107 us -> 0 us
  blocking collectives: 37.6 us -> 0 us
  between operations: 15.6 us -> 0.66 us
    pallas_call x0 -> x4, Pallas kernels: none -> 385 us  [the longest x2 291 us: iterate(): pl.pallas_call(functools.partial(iterate_kernel, rows, cols, units, block...]
    psum x4 -> x0, waiting for transfers between devices: 260 us -> none  [the longest x2 155 us: shards(): gram_sum = lax.psum(self_gram(left_sum), 'row')]
    another operation x40 -> x0, other arithmetic: 183 us -> none  [the longest x24 99.1 us: solve_rows(): corner = lax.linalg.cholesky(trailing[:size, :size], symmetrize_input=False)]
    reduce_scatter x2 -> x0, waiting for transfers between devices: 178 us -> none  [shards(): lax.psum_scatter(transposed, 'row', scatter_dimension=1, tiled=True)]
    all_gather x3 -> x0, waiting for transfers between devices: 174 us -> none  [the longest x2 101 us: shards(): lax.all_gather(products, 'row', axis=1, tiled=True)]
    dot_general x34 -> x0, matrix products: 105 us -> none  [the longest x2 24.1 us: shards(): partials = jnp.dot(blended, right_full, precision=wide_mode)]
    unnamed x2 -> x0, blocking collectives: 25.4 us -> none
    psum x2 -> x0, blocking collectives: 12.2 us -> none  [shards(): lax.psum(jnp.sum(products * products, axis=0, keepdims=True), 'col')]
  transfers between devices with their start and end apart: 9 -> 0, of which waited for: 9 -> 0; matrix products, arithmetic and copies ran while one was open for 1% -> 0% of each run, Pallas kernels for 0% -> 0%
where the time goes in v2:
time: 389 us; the launch traced here: 388 us
  Pallas kernels  385 us (99%)
    pallas_call x2, Pallas kernels, iterate(): pl.pallas_call(functools.partial(iterate_kernel, rows, cols, units, block...  291 us
    pallas_call x1, Pallas kernels, gather(): pl.pallas_call(functools.partial(gather_kernel, rows, cols, blocks), name...  76.8 us
    pallas_call x1, Pallas kernels, outputs(): pl.pallas_call(functools.partial(final_kernel, scale_factor), name='outpu...  17.4 us

profile of v2, /device:TPU:13, one launch (start us, length us, event | category | flops | bytes accessed | tf_op | source)
XLA Modules:
  0.0 388.5 jit_solution(18333617035083756133)
XLA Ops:
  0.6 150.9 %iterate.2 = (bf16[1024,2048]{1,0:T(8,128)(2,1)}, bf16[1024,2048]{1,0:T(8,128)(2,1)}, f32[2,2,4,32,1024]{4,3,2,1,0:T(8,128)}, f32[2,32,2048]{2,1,0:T(8,128)}, f32[2,2,4,2,16,512]{5,4,3,2,1,0:T(8,128)}) custom-call(f32[64,2048]{1,0:T(8,128)} %bitcast.9, f32[1024,2048]{1,0:T(8,128)} %m.1, bf16[1024,2048]{1,0:T(8,128)(2,1)} %g.1), custom_call_target="tpu_custom_call" | custom-call | flops 60000002048 | bytes 25165824 | tf_op jit(solution)/shard_map/iterate/pallas_call | solution.py:546
  151.6 139.9 %iterate.3 = (f32[2,2,4,32,1024]{4,3,2,1,0:T(8,128)}, f32[2,32,2048]{2,1,0:T(8,128)}, f32[2,2,4,2,16,512]{5,4,3,2,1,0:T(8,128)}) custom-call(f32[2,32,2048]{2,1,0:T(8,128)} %get-tuple-element.16.refs_0_, f32[512,512]{1,0:T(8,128)} %bitcast.12, bf16[1024,2048]{1,0:T(8,128)(2,1)} %get-tuple-element.18.refs_2_, bf16[1024,2048]{1,0:T(8,128)(2,1)} %get-tuple-element.19.refs_3_), custom_call_target="tpu_custom_call" | custom-call | flops 60000002048 | bytes 25165824 | tf_op jit(solution)/shard_map/iterate/pallas_call | solution.py:546
  291.5 76.8 %gather.1 = (f32[512,2048]{1,0:T(8,128)}, f32[8,512]{1,0:T(8,128)}, bf16[1024,512]{1,0:T(8,128)(2,1)}, bf16[1024,512]{1,0:T(8,128)(2,1)}) custom-call(f32[64,2048]{1,0:T(8,128)} %bitcast.13, f32[512,512]{1,0:T(8,128)} %bitcast.11, f32[512,1024]{1,0:T(8,128)} %bitcast.10), custom_call_target="tpu_custom_call" | custom-call | flops 30000001024 | bytes 16777216 | tf_op jit(solution)/shard_map/gather/pallas_call | solution.py:687
  368.3 17.4 %outputs.1 = (f32[1024,2048]{1,0:T(8,128)}, bf16[1024,2048]{1,0:T(8,128)(2,1)}) custom-call(bf16[1024,512]{1,0:T(8,128)(2,1)} %get-tuple-element.23.high, bf16[1024,512]{1,0:T(8,128)(2,1)} %get-tuple-element.24.low, f32[512,2048]{1,0:T(8,128)} %get-tuple-element.25.q, f32[8,512]{1,0:T(8,128)} %get-tuple-element.26.norms, f32[1024,2048]{1,0:T(8,128)} %m.1, ...), custom_call_target="tpu_custom_call" | custom-call | flops 8589934592 | bytes 29360128 | tf_op jit(solution)/shard_map/outputs/pallas_call | solution.py:122
  385.8 0.7 slice.3
  386.5 0.1 dynamic-slice_bitcast_fusion
  386.6 1.9 divide_bitcast_fusion

commit v3 on v2

--- a/solution.py
+++ b/solution.py
@@ -15,6 +15,7 @@
 exact = lax.Precision.HIGHEST
 f32, bf16 = jnp.float32, jnp.bfloat16
 VMEM = pl.BlockSpec(memory_space=pltpu.VMEM)
+FAR = pl.BlockSpec(memory_space=pl.ANY)
 MESH = pl.DeviceIdType.MESH
 LIMIT = 56 << 20
 
@@ -102,18 +103,22 @@
     return jnp.broadcast_to(column, (rank, 128)).T[:8, :]
 
 
-def final_kernel(scale_factor, high, low, q, norms, m, g, weight, new_m, new_w):
+def final_kernel(scale_factor, high, low, q, norms, m, g, weight, new_m, new_w, new_r, scaled):
     rank = q.shape[0]
     column = jnp.broadcast_to(norms[0:1, :], (128, rank)).T[:, 0:1]
     s = q[...]
     left = (high[...], low[...])
     blended = m[...] + g[...].astype(f32)
     new_m[...] = blended - (1.0 - momentum_decay) * nn(left[0], s.astype(bf16))
-    update = three(nn, left, split(s / column))
+    right = s / column
+    scaled[...] = right
+    size = new_r.shape[0]
+    new_r[...] = scaled[pl.ds(pl.multiple_of(lax.axis_index("row") * size, size), size), :]
+    update = three(nn, left, split(right))
     new_w[...] = (weight[...].astype(f32) - scale_factor * update).astype(bf16)
 
 
-def outputs(scale_factor, high, low, q, norms, momentum, gradient, weight):
+def outputs(scale_factor, size, high, low, q, norms, momentum, gradient, weight):
     rank, cols = q.shape
     rows = high.shape[0]
     wide = min(256, cols)
@@ -124,8 +129,13 @@
         name="outputs",
         grid=(cols // wide,),
         in_specs=[side, side, pl.BlockSpec((rank, wide), lambda j: (0, j)), pl.BlockSpec((8, rank), lambda j: (0, 0)), block, block, block],
-        out_specs=[block, block],
-        out_shape=[jax.ShapeDtypeStruct((rows, cols), f32), jax.ShapeDtypeStruct((rows, cols), bf16)],
+        out_specs=[block, block, pl.BlockSpec((size, wide), lambda j: (0, j))],
+        out_shape=[
+            jax.ShapeDtypeStruct((rows, cols), f32),
+            jax.ShapeDtypeStruct((rows, cols), bf16),
+            jax.ShapeDtypeStruct((size, cols), f32),
+        ],
+        scratch_shapes=[pltpu.VMEM((rank, wide), f32)],
         compiler_params=pltpu.CompilerParams(vmem_limit_bytes=LIMIT),
         cost_estimate=cost(8 * rank * rows * cols, 14 * rows * cols),
     )(high, low, q, norms, momentum, gradient, weight)
@@ -192,12 +202,13 @@
 
 def iterate_kernel(rows, cols, units, blocks, mode, *refs):
     if mode == 0:
-        own, m, g, high, low, out, chunk, gall = refs[:8]
-        refs = refs[8:]
+        own, m_far, g_far, high_far, low_far, out, chunk, gall = refs[:8]
+        m, g, high, low, in_sem, out_sem = refs[8:14]
+        refs = refs[14:]
     else:
-        own, gram, high, low, out, chunk, gall = refs[:7]
-        x, xh, xl, a, w, work, total, sq, sq_in, ss, sr = refs[7:18]
-        refs = refs[18:]
+        own, gram, high_far, low_far, out, chunk, gall = refs[:7]
+        x, xh, xl, a, w, work, total, sq, sq_in, ss, sr, high, low, in_sem = refs[7:21]
+        refs = refs[21:]
     whole, part, half, near, far, gram_own, ph, pw, q, qy, h, hz, gq, gyr, gh, gzr, zs, zr, ys, yr = refs[:20]
     join_s, join_r, far_s, far_r, back_s, back_r, qy_s, qy_r, hz_s, hz_r, send, recv = refs[20:]
     at = Place(rows, cols)
@@ -222,6 +233,18 @@
     def loop(start, count, body):
         lax.fori_loop(start, count, lambda j, c: (body(j), c)[1], 0)
 
+    split_lines = high.shape[0] // units
+
+    def fetch(j):
+        span = spread(j, split_lines)
+        pairs = ((m_far, m), (g_far, g)) if mode == 0 else ((high_far, high), (low_far, low))
+        return [pltpu.make_async_copy(src.at[span], dst.at[span], in_sem.at[j, i]) for i, (src, dst) in enumerate(pairs)]
+
+    def keep(j):
+        span = spread(j, split_lines)
+        pairs = ((high, high_far), (low, low_far))
+        return [pltpu.make_async_copy(src.at[span], dst.at[span], out_sem.at[j, i]) for i, (src, dst) in enumerate(pairs)]
+
     def lanes(u):
         return spread(u % step_lanes, wide) if mode else spread(u, wide)
 
@@ -240,6 +263,9 @@
             z_copy(u, d).start()
         for e in range(1, at.flat):
             y_copy(u, e, 0).start()
+    for u in range(units):
+        for copy in fetch(u):
+            copy.start()
     for u in range(units):
         whole[u, at.z, at.y] = own[u // step_lanes, :, lanes(u)] if mode else own[:, lanes(u)]
 
@@ -360,11 +386,13 @@
         return u % step_lanes if mode else u
 
     if mode == 0:
-        count = m.shape[0] // units
-
         def divide(j):
-            span = spread(j, count)
+            span = spread(j, split_lines)
+            for copy in fetch(j):
+                copy.wait()
             high[span, :], low[span, :] = split(m[span, :] + g[span, :].astype(f32))
+            for copy in keep(j):
+                copy.start()
 
         loop(0, units, divide)
         forward(0)
@@ -393,6 +421,9 @@
         loop(0, units, step)
         xh[...], xl[...] = split(x[...])
         total[...] = jnp.zeros_like(total)
+        for u in range(units):
+            for copy in fetch(u):
+                copy.wait()
 
         def solve(r, u):
             arrived(u)
@@ -466,6 +497,9 @@
     go.drain()
 
     def finish(u):
+        if mode == 0:
+            for copy in keep(u):
+                copy.wait()
         for d in range(1, at.deep):
             z_copy(u, d).wait_send()
         for e in range(1, at.flat):
@@ -515,12 +549,14 @@
     scratch = []
     if mode == 0:
         out_shape = [jax.ShapeDtypeStruct((lines, width), bf16)] * 2 + out_shape
+        scratch = [pltpu.VMEM((lines, width), dtype) for dtype in (f32, bf16, bf16, bf16)] + [dma((units, 2))] * 2
     else:
         block = rank // units
         scratch = [pltpu.VMEM((rank, rank), f32)] + [pltpu.VMEM((rank, rank), bf16)] * 2
         scratch += [pltpu.VMEM((block, block), f32)] * 2 + [pltpu.VMEM((rank, rank), f32), pltpu.VMEM((2, half_rank, 128), f32)]
         scratch += [pltpu.VMEM((2, 8, half_rank), f32), pltpu.VMEM((2, cols - 1, 8, half_rank), f32)]
         scratch += [dma((2, cols - 1))] * 2
+        scratch += [pltpu.VMEM((lines, width), bf16)] * 2 + [dma((units, 2))]
     scratch += [
         pltpu.VMEM((units, deep, flat, size, wide), f32),
         pltpu.VMEM((2, CORES, PIECES, piece, lines), f32),
@@ -547,8 +583,8 @@
         functools.partial(iterate_kernel, rows, cols, units, blocks, mode),
         name="iterate",
         out_shape=out_shape,
-        in_specs=[VMEM] * (1 + len(args)),
-        out_specs=[VMEM] * len(out_shape),
+        in_specs=[VMEM] * (len(args) - 1) + [FAR] * 2,
+        out_specs=[FAR] * (len(out_shape) - 3) + [VMEM] * 3,
         scratch_shapes=scratch,
         compiler_params=pltpu.CompilerParams(collective_id=ident, has_side_effects=True, vmem_limit_bytes=LIMIT),
         cost_estimate=cost(6e10, 24 << 20),
@@ -558,8 +594,9 @@
 
 
 def gather_kernel(rows, cols, blocks, *refs):
-    own, gram, p, solved, norms, left_high, left_low = refs[:7]
-    whole, x, xh, xl, a, w, work, total, sq, sq_in, ss, sr, zs, zr, ys, yr = refs[7:]
+    own, gram, p_far, solved_far, norms, left_high_far, left_low_far = refs[:7]
+    whole, x, xh, xl, a, w, work, total, sq, sq_in, ss, sr = refs[7:19]
+    p, solved, left_high, left_low, p_sem, solved_sem, left_sem, zs, zr, ys, yr = refs[19:]
     at = Place(rows, cols)
     col_peers = [(at.row, (at.col + d) % cols) for d in range(1, cols)]
     greet(at.y_peers() + at.z_peers() + col_peers)
@@ -597,6 +634,8 @@
             z_copy(j, d).start()
         for e in range(1, at.flat):
             y_copy(j, e, 0).start()
+    fetch = pltpu.make_async_copy(p_far, p, p_sem.at[0])
+    fetch.start()
     for j in range(blocks):
         whole[j, at.z, at.y] = own[:, lanes(j)]
 
@@ -618,21 +657,38 @@
     work[...] = gram[...]
     x[...] = eye(rank)
 
-    def step(j):
-        factor_step(j, work, x, a, w)
-
-        @pl.when(j > 0)
+    steps = rank // a.shape[0]
+    each = blocks // steps
+
+    def step(i):
+        factor_step(i, work, x, a, w)
+
+        @pl.when(i > 0)
         def _():
-            forward(j - 1)
-
-    loop(blocks, step)
+            for k in range(each):
+                forward((i - 1) * each + k)
+
+    loop(steps, step)
     xh[...], xl[...] = split(x[...])
     lines = min(256, p.shape[1])
+    fetch.wait()
+
+    def left_out(i):
+        span = pl.ds(pl.multiple_of(i * lines, lines), lines)
+        return [
+            pltpu.make_async_copy(left_high.at[span], left_high_far.at[span], left_sem.at[i, 0]),
+            pltpu.make_async_copy(left_low.at[span], left_low_far.at[span], left_sem.at[i, 1]),
+        ]
+
+    def solved_out(j):
+        return pltpu.make_async_copy(solved.at[:, lanes(j)], solved_far.at[:, lanes(j)], solved_sem.at[j])
 
     def left(i):
         span = pl.ds(pl.multiple_of(i * lines, lines), lines)
         value = three(nn, (xh[...], xl[...]), split(p[:, span])).T
         left_high[span, :], left_low[span, :] = split(value)
+        for copy in left_out(i):
+            copy.start()
 
     loop(p.shape[1] // lines, left)
     total[...] = jnp.zeros_like(total)
@@ -644,13 +700,12 @@
             sums = sums + s[:, k : k + 128] * s[:, k : k + 128]
         total[...] = sums
         solved[:, lanes(j)] = s
-
-        @pl.when(j == min(1, blocks - 1))
+        solved_out(j).start()
+
+        @pl.when((j >= 1) & (j <= each))
         def _():
-            forward(blocks - 1)
-
-    if blocks == 1:
-        forward(0)
+            forward((steps - 1) * each + j - 1)
+
     loop(blocks, turn)
     sq[...] = row_sums(total[...])
     go = Sender(ss, sr)
@@ -661,6 +716,11 @@
         value = value + sq_in[d]
     norms[...] = jnp.sqrt(value + epsilon)
     go.drain()
+    for i in range(p.shape[1] // lines):
+        for copy in left_out(i):
+            copy.wait()
+    for j in range(blocks):
+        solved_out(j).wait()
     for j in range(blocks):
         for d in range(1, at.deep):
             z_copy(j, d).wait_send()
@@ -672,10 +732,10 @@
 def gather(rows, cols, ident, own, gram, p):
     size, width = own.shape
     rank, lines = p.shape
-    blocks = max(1, min(4, width // 256, rank // 128))
+    blocks = max(1, min(8, width // 256))
     deep = outer_factor(rows)
     flat = rows // deep
-    block = rank // blocks
+    block = min(128, rank)
     dma = pltpu.SemaphoreType.DMA
     out_shape = [jax.ShapeDtypeStruct((rank, width), f32), jax.ShapeDtypeStruct((8, rank), f32)]
     out_shape += [jax.ShapeDtypeStruct((lines, rank), bf16)] * 2
@@ -683,13 +743,15 @@
     scratch += [pltpu.VMEM((rank, rank), f32)] + [pltpu.VMEM((rank, rank), bf16)] * 2
     scratch += [pltpu.VMEM((block, block), f32)] * 2 + [pltpu.VMEM((rank, rank), f32), pltpu.VMEM((rank, 128), f32)]
     scratch += [pltpu.VMEM((8, rank), f32), pltpu.VMEM((cols - 1, 8, rank), f32)] + [dma((cols - 1,))] * 2
+    scratch += [pltpu.VMEM((rank, lines), f32), pltpu.VMEM((rank, width), f32)] + [pltpu.VMEM((lines, rank), bf16)] * 2
+    scratch += [dma((1,)), dma((blocks,)), dma((lines // min(256, lines), 2))]
     scratch += [dma((blocks, deep - 1))] * 2 + [dma((blocks, flat - 1, deep))] * 2
     return pl.pallas_call(
         functools.partial(gather_kernel, rows, cols, blocks),
         name="gather",
         out_shape=out_shape,
-        in_specs=[VMEM] * 3,
-        out_specs=[VMEM] * len(out_shape),
+        in_specs=[VMEM, VMEM, FAR],
+        out_specs=[FAR, VMEM, FAR, FAR],
         scratch_shapes=scratch,
         compiler_params=pltpu.CompilerParams(collective_id=ident, has_side_effects=True, vmem_limit_bytes=LIMIT),
         cost_estimate=cost(3e10, 16 << 20),
@@ -705,12 +767,10 @@
     own = own.reshape(rank // rows, own.shape[-1])
     products, norms, left_high, left_low = gather(rows, cols, 2, own, gram, joined)
     scale_factor = step_rate * (out_dim * in_dim / rank) ** 0.5
-    new_momentum, new_weight = outputs(scale_factor, left_high, left_low, products, norms, momentum, gradient, weight)
-    size = rank // rows
-    start = lax.axis_index("row") * size
-    some = lax.dynamic_slice_in_dim(products, start, size, axis=0)
-    norm = lax.dynamic_slice_in_dim(norms[0], start, size, axis=0)
-    return new_momentum, new_weight, (some / norm[:, None]).T
+    new_momentum, new_weight, new_right = outputs(
+        scale_factor, rank // rows, left_high, left_low, products, norms, momentum, gradient, weight
+    )
+    return new_momentum, new_weight, new_right.T
 
 
 def solution(mesh):

time: 389 us -> 375 us (0.964)
  Pallas kernels: 385 us -> 374 us
    pallas_call x2, Pallas kernels: 291 us -> 282 us  [iterate(): pl.pallas_call(functools.partial(iterate_kernel, rows, cols, units, block...]
where the time goes in v3:
time: 375 us
  Pallas kernels  374 us (100%)
    pallas_call x2, Pallas kernels, iterate(): pl.pallas_call(functools.partial(iterate_kernel, rows, cols, units, block...  282 us
    pallas_call x1, Pallas kernels, gather(): pl.pallas_call(functools.partial(gather_kernel, rows, cols, blocks), name...  74.3 us
    pallas_call x1, Pallas kernels, outputs(): pl.pallas_call(functools.partial(final_kernel, scale_factor), name='outpu...  17.5 us

profile of v3, /device:TPU:13, one launch (start us, length us, event | category | flops | bytes accessed | tf_op | source)
XLA Modules:
  0.0 374.8 jit_solution(2681426276886373717)
XLA Ops:
  0.6 144.9 %iterate.2 = (bf16[1024,2048]{1,0:T(8,128)(2,1)}, bf16[1024,2048]{1,0:T(8,128)(2,1)}, f32[2,2,4,32,1024]{4,3,2,1,0:T(8,128)}, f32[2,32,2048]{2,1,0:T(8,128)}, f32[2,2,4,2,16,512]{5,4,3,2,1,0:T(8,128)}) custom-call(f32[64,2048]{1,0:T(8,128)} %bitcast.6, f32[1024,2048]{1,0:T(8,128)} %m.1, bf16[1024,2048]{1,0:T(8,128)(2,1)} %g.1), custom_call_target="tpu_custom_call" | custom-call | flops 60000002048 | bytes 25165824 | tf_op jit(solution)/shard_map/iterate/pallas_call | solution.py:582
  145.5 137.5 %iterate.3 = (f32[2,2,4,32,1024]{4,3,2,1,0:T(8,128)}, f32[2,32,2048]{2,1,0:T(8,128)}, f32[2,2,4,2,16,512]{5,4,3,2,1,0:T(8,128)}) custom-call(f32[2,32,2048]{2,1,0:T(8,128)} %get-tuple-element.17.refs_0_, f32[512,512]{1,0:T(8,128)} %bitcast.9, bf16[1024,2048]{1,0:T(8,128)(2,1)} %get-tuple-element.19.refs_2_, bf16[1024,2048]{1,0:T(8,128)(2,1)} %get-tuple-element.20.refs_3_), custom_call_target="tpu_custom_call" | custom-call | flops 60000002048 | bytes 25165824 | tf_op jit(solution)/shard_map/iterate/pallas_call | solution.py:582
  283.0 74.3 %gather.1 = (f32[512,2048]{1,0:T(8,128)}, f32[8,512]{1,0:T(8,128)}, bf16[1024,512]{1,0:T(8,128)(2,1)}, bf16[1024,512]{1,0:T(8,128)(2,1)}) custom-call(f32[64,2048]{1,0:T(8,128)} %bitcast.10, f32[512,512]{1,0:T(8,128)} %bitcast.8, f32[512,1024]{1,0:T(8,128)} %bitcast.7), custom_call_target="tpu_custom_call" | custom-call | flops 30000001024 | bytes 16777216 | tf_op jit(solution)/shard_map/gather/pallas_call | solution.py:749
  357.3 17.5 %outputs.1 = (f32[1024,2048]{1,0:T(8,128)}, bf16[1024,2048]{1,0:T(8,128)(2,1)}, f32[64,2048]{1,0:T(8,128)}) custom-call(bf16[1024,512]{1,0:T(8,128)(2,1)} %get-tuple-element.24.high, bf16[1024,512]{1,0:T(8,128)(2,1)} %get-tuple-element.25.low, f32[512,2048]{1,0:T(8,128)} %get-tuple-element.26.q, f32[8,512]{1,0:T(8,128)} %get-tuple-element.27.norms, ...), custom_call_target="tpu_custom_call" | custom-call | flops 8589934592 | bytes 29360128 | tf_op jit(solution)/shard_map/outputs/pallas_call | solution.py:127

commit v4 on v3

--- a/solution.py
+++ b/solution.py
@@ -202,8 +202,8 @@
 
 def iterate_kernel(rows, cols, units, blocks, mode, *refs):
     if mode == 0:
-        own, m_far, g_far, high_far, low_far, out, chunk, gall = refs[:8]
-        m, g, high, low, in_sem, out_sem = refs[8:14]
+        own, m_far, g_far, high_far, low_far, chunk, gall = refs[:7]
+        out, m, g, high, low, in_sem, out_sem = refs[7:14]
         refs = refs[14:]
     else:
         own, gram, high_far, low_far, out, chunk, gall = refs[:7]
@@ -548,8 +548,9 @@
     ]
     scratch = []
     if mode == 0:
-        out_shape = [jax.ShapeDtypeStruct((lines, width), bf16)] * 2 + out_shape
-        scratch = [pltpu.VMEM((lines, width), dtype) for dtype in (f32, bf16, bf16, bf16)] + [dma((units, 2))] * 2
+        out_shape = [jax.ShapeDtypeStruct((lines, width), bf16)] * 2 + out_shape[1:]
+        scratch = [pltpu.VMEM((2, CORES, PIECES, piece, lines), f32)]
+        scratch += [pltpu.VMEM((lines, width), dtype) for dtype in (f32, bf16, bf16, bf16)] + [dma((units, 2))] * 2
     else:
         block = rank // units
         scratch = [pltpu.VMEM((rank, rank), f32)] + [pltpu.VMEM((rank, rank), bf16)] * 2
@@ -584,13 +585,13 @@
         name="iterate",
         out_shape=out_shape,
         in_specs=[VMEM] * (len(args) - 1) + [FAR] * 2,
-        out_specs=[FAR] * (len(out_shape) - 3) + [VMEM] * 3,
+        out_specs=[VMEM] * 3 if mode else [FAR] * 2 + [VMEM] * 2,
         scratch_shapes=scratch,
         compiler_params=pltpu.CompilerParams(collective_id=ident, has_side_effects=True, vmem_limit_bytes=LIMIT),
         cost_estimate=cost(6e10, 24 << 20),
     )(own, *args)
-    joined, chunk, gall = res[-3:]
-    return list(res[:-3]) + [joined.reshape(rank, lines), chunk, gall.reshape(rank, rank)]
+    first = [res[0].reshape(rank, lines)] if mode else list(res[:2])
+    return first + [res[-2], res[-1].reshape(rank, rank)]
 
 
 def gather_kernel(rows, cols, blocks, *refs):
@@ -761,7 +762,7 @@
 def shards(rows, cols, momentum, gradient, weight, right_start):
     out_dim, in_dim = momentum.shape[0] * rows, momentum.shape[1] * cols
     rank = right_start.shape[1] * rows
-    high, low, joined, own, gram = iterate(0, rows, cols, 0, right_start.T, momentum, gradient)
+    high, low, own, gram = iterate(0, rows, cols, 0, right_start.T, momentum, gradient)
     for iteration in range(1, ITERS):
         joined, own, gram = iterate(1, rows, cols, 1, own, gram, high, low)
     own = own.reshape(rank // rows, own.shape[-1])

time: 375 us -> 375 us (level)
  no operation moved by 1% of the time
where the time goes in v4:
time: 375 us; the launch traced here: 374 us
  Pallas kernels  374 us (100%)
    pallas_call x2, Pallas kernels, iterate(): pl.pallas_call(functools.partial(iterate_kernel, rows, cols, units, block...  282 us
    pallas_call x1, Pallas kernels, gather(): pl.pallas_call(functools.partial(gather_kernel, rows, cols, blocks), name...  74.3 us
    pallas_call x1, Pallas kernels, outputs(): pl.pallas_call(functools.partial(final_kernel, scale_factor), name='outpu...  17.5 us

profile of v4, /device:TPU:13, one launch (start us, length us, event | category | flops | bytes accessed | tf_op | source)
XLA Modules:
  0.0 374.2 jit_solution(621798966529077344)
XLA Ops:
  0.6 144.2 %iterate.2 = (bf16[1024,2048]{1,0:T(8,128)(2,1)}, bf16[1024,2048]{1,0:T(8,128)(2,1)}, f32[2,32,2048]{2,1,0:T(8,128)}, f32[2,2,4,2,16,512]{5,4,3,2,1,0:T(8,128)}) custom-call(f32[64,2048]{1,0:T(8,128)} %bitcast.6, f32[1024,2048]{1,0:T(8,128)} %m.1, bf16[1024,2048]{1,0:T(8,128)(2,1)} %g.1), custom_call_target="tpu_custom_call" | custom-call | flops 60000002048 | bytes 25165824 | tf_op jit(solution)/shard_map/iterate/pallas_call | solution.py:583
  144.9 137.5 %iterate.3 = (f32[2,2,4,32,1024]{4,3,2,1,0:T(8,128)}, f32[2,32,2048]{2,1,0:T(8,128)}, f32[2,2,4,2,16,512]{5,4,3,2,1,0:T(8,128)}) custom-call(f32[2,32,2048]{2,1,0:T(8,128)} %get-tuple-element.17.refs_0_, f32[512,512]{1,0:T(8,128)} %bitcast.9, bf16[1024,2048]{1,0:T(8,128)(2,1)} %get-tuple-element.19.refs_2_, bf16[1024,2048]{1,0:T(8,128)(2,1)} %get-tuple-element.20.refs_3_), custom_call_target="tpu_custom_call" | custom-call | flops 60000002048 | bytes 25165824 | tf_op jit(solution)/shard_map/iterate/pallas_call | solution.py:583
  282.4 74.3 %gather.1 = (f32[512,2048]{1,0:T(8,128)}, f32[8,512]{1,0:T(8,128)}, bf16[1024,512]{1,0:T(8,128)(2,1)}, bf16[1024,512]{1,0:T(8,128)(2,1)}) custom-call(f32[64,2048]{1,0:T(8,128)} %bitcast.10, f32[512,512]{1,0:T(8,128)} %bitcast.8, f32[512,1024]{1,0:T(8,128)} %bitcast.7), custom_call_target="tpu_custom_call" | custom-call | flops 30000001024 | bytes 16777216 | tf_op jit(solution)/shard_map/gather/pallas_call | solution.py:750
  356.6 17.5 %outputs.1 = (f32[1024,2048]{1,0:T(8,128)}, bf16[1024,2048]{1,0:T(8,128)(2,1)}, f32[64,2048]{1,0:T(8,128)}) custom-call(bf16[1024,512]{1,0:T(8,128)(2,1)} %get-tuple-element.24.high, bf16[1024,512]{1,0:T(8,128)(2,1)} %get-tuple-element.25.low, f32[512,2048]{1,0:T(8,128)} %get-tuple-element.26.q, f32[8,512]{1,0:T(8,128)} %get-tuple-element.27.norms, ...), custom_call_target="tpu_custom_call" | custom-call | flops 8589934592 | bytes 29360128 | tf_op jit(solution)/shard_map/outputs/pallas_call | solution.py:127
